TPU v7x, 512 devices: a whole 4x4x16 slice. The times are simulated.
512 devices in a mesh: row: 16 (over x_hi, y, core), col: 32 (over x_lo, z).
Axes of the slice: x: 4 (x_hi: 2, x_lo: 2; x = x_hi * 2 + x_lo), y: 4, z: 16, core: 2. Of those that a mesh axis runs over, the one named last changes fastest.
Arguments:
- blocks: bfloat16 [1536, 64, 4096], P('col', 'row'), may hold values from -1.75 to 1.75
- columns: int32 [1536, 64], P('col', 'row'), may hold values from 0 to 95, as said below
- counts: int32 [1536, 16], P('col', 'row'), may hold values from 0 to 4, as said below
Outputs:
- product: bfloat16 [1536, 64, 4096], P('col', 'row')
Inputs may be any that keep to these rules, and one draw needn't show every extreme that they name: `counts`: in each tile, every block row has between 0 and 4 live slots; in every tile some block row has exactly 4. The live slots of a block row name different tile columns, at most 2 of them below 48 and at most 2 at or above; in every tile some block row reaches 2 in both halves. A live tile column t of global block row g satisfies (t - g) mod 48 < 8. Dead slots hold arbitrary values in the range.
All inputs are finite; a program needn't handle non-finite values.
Results may differ from a plain program's by a relative error of at most 0.001.
Values may be sent and summed in bfloat16 or wider, within the bound.
No kernel may reach another device: no remote copies, remote signals or barrier semaphores. Data moves between devices by JAX's collectives and lax.ppermute only.
A program may use at most 128 MiB of HBM per device.

v0:
```python
import jax
import jax.numpy as jnp
from jax import lax
from jax.sharding import PartitionSpec as P

BLK = 64
HS = 2
SECTIONS = 2


def broadcast(block, axis, owner):
    block = jnp.where(lax.axis_index(axis) == owner, block, jnp.zeros_like(block))
    return lax.psum(block, axis)


def from_behind(block, axis, distance):
    devices = range(lax.axis_size(axis))
    route = [((i - distance) % len(devices), i) for i in devices]
    return lax.ppermute(block, axis, route)


def compact(tile_blocks, tile_cols, tile_count, half_index):
    strip_count = tile_cols.shape[0]
    slot_count = tile_cols.shape[1]
    slot_ids = jnp.arange(slot_count, dtype=jnp.int32)
    live_slots = (slot_ids[None, :] < tile_count[:, None]) & (
        tile_cols // strip_count == half_index
    )
    position = jnp.cumsum(live_slots.astype(jnp.int32), axis=1) - 1
    chosen = live_slots[:, :, None] & (
        position[:, :, None] == jnp.arange(HS, dtype=jnp.int32)[None, None, :]
    )
    picked = jnp.einsum(
        "isq,isx->iqx",
        chosen.astype(jnp.bfloat16),
        tile_blocks,
        preferred_element_type=jnp.bfloat16,
    )
    inner_rows = jnp.sum(
        jnp.where(chosen, (tile_cols - half_index * strip_count)[:, :, None], 0), axis=1
    ).astype(jnp.int32)
    used_flags = jnp.any(chosen, axis=1).astype(jnp.int32)
    return (picked, inner_rows, used_flags)


def section_term(
    picked, inner_rows, used_flags, right_blocks, right_cols, right_count, out_cols, out_live
):
    strip_count = picked.shape[0]
    slot_count = out_cols.shape[1]
    gathered = right_blocks[inner_rows]
    gathered_cols = right_cols[inner_rows]
    gathered_count = right_count[inner_rows]
    slot_ids = jnp.arange(slot_count, dtype=jnp.int32)
    right_live = slot_ids[None, None, :] < gathered_count[:, :, None]
    matches = (gathered_cols[:, :, :, None] == out_cols[:, None, None, :]) & right_live[
        :, :, :, None
    ]
    matches = matches & (used_flags[:, :, None, None] > 0) & out_live[:, None, None, :]
    selected = jnp.einsum(
        "iqbj,iqbx->iqjx",
        matches.astype(jnp.bfloat16),
        gathered,
        preferred_element_type=jnp.bfloat16,
    )
    left_blocks = picked.reshape(strip_count, HS, BLK, BLK)
    right_sel = selected.reshape(strip_count, HS, slot_count, BLK, BLK)
    contribution = jnp.einsum(
        "iqmn,iqjnp->ijmp", left_blocks, right_sel, preferred_element_type=jnp.float32
    )
    return contribution.reshape(strip_count, slot_count, BLK * BLK)


def local(blocks, columns, counts):
    count_now = counts[:, 0]
    strip_count = columns.shape[0]
    slot_count = columns.shape[1]
    out_live = jnp.arange(slot_count, dtype=jnp.int32)[None, :] < count_now[:, None]
    col_index = lax.axis_index("col")
    col_total = lax.axis_size("col")
    accumulated = jnp.zeros((strip_count, slot_count, blocks.shape[2]), jnp.float32)
    right_tile = (blocks, columns, count_now)
    for section in range(SECTIONS):
        target_piece = (col_index + section) % col_total
        root_index = target_piece // 2
        half_index = target_piece % 2
        got_blocks, got_cols, got_count = (
            broadcast(blocks, "row", root_index),
            broadcast(columns, "row", root_index),
            broadcast(count_now, "row", root_index),
        )
        picked, inner_rows, used_flags = compact(got_blocks, got_cols, got_count, half_index)
        if section > 0:
            right_tile = from_behind((right_tile[0], right_tile[1], right_tile[2]), "col", -1)
        accumulated = accumulated + section_term(
            picked,
            inner_rows,
            used_flags,
            right_tile[0],
            right_tile[1],
            right_tile[2],
            columns,
            out_live,
        )
    return accumulated.astype(jnp.bfloat16)


def solution(mesh):
    return jax.shard_map(
        local,
        mesh=mesh,
        in_specs=(P("col", "row", None), P("col", "row"), P("col", "row")),
        out_specs=P("col", "row", None),
        check_vma=False,
    )
```

profile of v0, /device:TPU:1, one launch (start us, length us, event | category | flops | bytes accessed | tf_op | source)
XLA Modules:
  0.0 228.3 jit_solution(16284222606765548050)
XLA Ops:
  6.5 12.9 %collective-permute-start.2 = (bf16[48,4,4096]{2,1,0:T(4,128)(2,1)}, bf16[48,4,4096]{2,1,0:T(4,128)(2,1)S(1)}, u32[]{:S(2)}, u32[]{:S(2)}) collective-permute-start(bf16[48,4,4096]{2,1,0:T(4,128)(2,1)} %param.3), channel_id=1, source_target_pairs={{1,0},{2,1},{3,2},{4,3},{5,4},{6,5},{7,6},{8,7},{9,8},{10,9},{11,1... | collective-permute-start | bytes 4718600 | tf_op jit(solution)/shard_map/ppermute | solution.py:19
  20.2 2.6 %collective-permute-start = (s32[48,4]{1,0:T(8,128)S(1)}, s32[48,4]{1,0:T(8,128)S(1)}, u32[]{:S(2)}, u32[]{:S(2)}) collective-permute-start(s32[48,4]{1,0:T(8,128)S(1)} %copy.37), channel_id=1, source_target_pairs={{1,0},{2,1},{3,2},{4,3},{5,4},{6,5},{7,6},{8,7},{9,8},{10,9},{11,1... | collective-permute-start | bytes 2312 | tf_op jit(solution)/shard_map/ppermute | solution.py:19
  22.8 2.6 %collective-permute-start.1 = (s32[48]{0:T(128)}, s32[48]{0:T(128)S(1)}, u32[]{:S(2)}, u32[]{:S(2)}) collective-permute-start(s32[48]{0:T(128)} %bitcast.53), channel_id=1, source_target_pairs={{1,0},{2,1},{3,2},{4,3},{5,4},{6,5},{7,6},{8,7},{9,8},{10,9},{11,1... | collective-permute-start | bytes 584 | tf_op jit(solution)/shard_map/ppermute | solution.py:19
  25.6 4.4 %broadcast_select_fusion = (bf16[48,4,4096]{2,1,0:T(4,128)(2,1)}, bf16[48,4,4096]{2,1,0:T(4,128)(2,1)}) fusion(bf16[48,4,4096]{2,1,0:T(4,128)(2,1)} %param.3, pred[]{:T(512)S(6)} %eq.86, pred[]{:T(512)S(6)} %eq.39), kind=kLoop, calls=%fused_computation.12 | loop fusion | flops 1572864 | bytes 4718594 | tf_op jit(solution)/shard_map/jit(_where)/select_n | solution.py:12
  30.0 12.7 %all-reduce = (s32[48,4]{0,1:T(4,128)S(1)}, s32[48]{0:T(128)S(1)}, s32[48,4]{0,1:T(4,128)S(1)}, s32[48]{0:T(128)S(1)}) all-reduce(s32[48,4]{0,1:T(4,128)S(1)} %get-tuple-element.22, s32[48]{0:T(128)S(1)} %get-tuple-element.24, s32[48,4]{0,1:T(4,128)S(1)} %get-tuple-element.21, ...), channel_id=1, replica_groups=mesh['row'=16,'col'=32] {'row'}, use_global_device_ids=true, to_apply=%region_1.2 | all-reduce | flops 480 | bytes 3840 | tf_op jit(solution)/shard_map/psum | solution.py:13
  43.4 1.7 fusion.31
  45.1 0.9 select_reduce_fusion.1
  46.3 7.4 %gather_fusion.2 = bf16[96,4,4096]{2,1,0:T(4,128)(2,1)} fusion(bf16[48,4,4096]{2,1,0:T(4,128)(2,1)S(1)} %copy-done.1, s32[1024]{0:T(1024)S(1)} %pad_clamp_fusion.1), kind=kCustom, calls=%fused_computation.2 | custom fusion | bytes 6291840 | tf_op jit(solution)/shard_map/gather | solution.py:51
  54.3 1.2 gather_fusion.1
  57.2 5.5 %fusion.10 = bf16[48,2,4,4096]{3,2,1,0:T(4,128)(2,1)} fusion(bf16[48,2,4,4096]{3,2,1,0:T(4,128)(2,1)} %bitcast.58, s32[48,4]{1,0:T(8,128)S(1)} %copy.37, s32[48,2,4]{2,1,0:T(2,128)S(1)} %bitcast.60, pred[48,4]{1,0:T(8,128)(4,1)S(1)} %iota_compare_fusion.2, pred[48,2]{1,0:T(8,128)(4,1)S(1)} %convert_compare_fusion.1, ...), kind=kOutput, calls=%fused_computation.19 | convolution fusion | flops 12589056 | bytes 6294432 | tf_op jit(solution)/shard_map/iqbj,iqbx->iqjx/dot_general | solution.py:60
  62.7 10.0 %reshape.101 = bf16[48,2,4,64,64]{4,3,2,1,0:T(8,128)(2,1)} reshape(bf16[48,2,4,4096]{3,2,1,0:T(4,128)(2,1)} %fusion.10) | data formatting | bytes 6291456 | tf_op jit(solution)/shard_map/reshape | solution.py:67
  72.8 1.2 gather_fusion.4
  74.9 7.3 %gather_fusion.5 = bf16[96,4,4096]{2,1,0:T(4,128)(2,1)} fusion(bf16[48,4,4096]{2,1,0:T(4,128)(2,1)S(1)} %collective-permute-done.2, s32[1024]{0:T(1024)S(1)} %pad_clamp_fusion), kind=kCustom, calls=%fused_computation.5 | custom fusion | bytes 6291840 | tf_op jit(solution)/shard_map/gather | solution.py:51
  82.1 5.5 %fusion.5 = bf16[48,2,4,4096]{3,2,1,0:T(4,128)(2,1)} fusion(bf16[48,2,4,4096]{3,2,1,0:T(4,128)(2,1)} %bitcast.59, s32[48,2,4]{2,1,0:T(2,128)S(1)} %bitcast.61, s32[48,4]{1,0:T(8,128)S(1)} %copy.37, pred[48,2]{1,0:T(8,128)(4,1)S(1)} %convert_compare_fusion, pred[48,2,4]{2,1,0:T(4,128)(4,1)S(1)} %iota_compare_fusion, pred[48,4]{1,0:T(8,128)(4,1)S(1)} %iota_compare_fusion.2), kind=kOutput, calls=%fused_computation.14 | convolution fusion | flops 12589056 | bytes 6294432 | tf_op jit(solution)/shard_map/iqbj,iqbx->iqjx/dot_general | solution.py:60
  87.6 10.0 %reshape.103 = bf16[48,2,4,64,64]{4,3,2,1,0:T(8,128)(2,1)} reshape(bf16[48,2,4,4096]{3,2,1,0:T(4,128)(2,1)} %fusion.5) | data formatting | bytes 6291456 | tf_op jit(solution)/shard_map/reshape | solution.py:67
  97.6 94.2 %all-reduce.4.cloned.1.call-done = (bf16[48,4,4096]{2,1,0:T(4,128)(2,1)}, bf16[48,4,4096]{2,1,0:T(4,128)(2,1)}) async-done(((bf16[48,4,4096]{2,1,0:T(4,128)(2,1)}, bf16[48,4,4096]{2,1,0:T(4,128)(2,1)}), (bf16[48,4,4096]{2,1,0:T(4,128)(2,1)}, bf16[48,4,4096]{2,1,0:T(4,128)(2,1)})) %all-reduce.4.cloned.1.call-update) | async-done | bytes 3145744 | tf_op jit(solution)/shard_map/psum | solution.py:13
  191.8 2.4 %fusion.37 = bf16[48,2,4096]{2,1,0:T(2,128)(2,1)S(1)} fusion(pred[48,4,2]{1,2,0:T(4,128)(4,1)S(1)} %get-tuple-element.26, bf16[48,4,4096]{2,1,0:T(4,128)(2,1)} %get-tuple-element.9), kind=kOutput, calls=%fused_computation.73 | convolution fusion | flops 3145728 | bytes 2359680 | tf_op jit(solution)/shard_map/isq,isx->iqx/dot_general | solution.py:33
  194.2 1.9 reshape.159
  196.1 2.4 %fusion.38 = bf16[48,2,4096]{2,1,0:T(2,128)(2,1)S(1)} fusion(pred[48,4,2]{1,2,0:T(4,128)(4,1)S(1)} %get-tuple-element.12, bf16[48,4,4096]{2,1,0:T(4,128)(2,1)} %get-tuple-element.10), kind=kOutput, calls=%fused_computation.74 | convolution fusion | flops 3145728 | bytes 2359680 | tf_op jit(solution)/shard_map/isq,isx->iqx/dot_general | solution.py:33
  198.5 1.9 reshape.161
  200.4 7.8 %fusion.3 = f32[48,4,64,64,1]{3,2,1,4,0:T(8,128)} fusion(bf16[48,2,4,64,64]{4,3,2,1,0:T(8,128)(2,1)} %reshape.101, bf16[48,2,64,64,1]{3,2,1,0,4:T(8,128)(2,1)} %reshape.159), kind=kOutput, calls=%fused_computation.10 | convolution fusion | flops 201326592 | bytes 7077888 | tf_op jit(solution)/shard_map/iqmn,iqjnp->ijmp/dot_general | solution.py:68
  208.3 6.5 %fusion.1 = bf16[48,4,64,64]{2,3,1,0:T(8,128)(2,1)} fusion(f32[48,4,64,64,1]{3,2,1,4,0:T(8,128)} %fusion.3, bf16[48,2,4,64,64]{4,3,2,1,0:T(8,128)(2,1)S(1)} %bitcast.57, bf16[48,2,64,64,1]{3,2,1,0,4:T(8,128)(2,1)S(1)} %copy-done.2), kind=kOutput, calls=%fused_computation.8 | convolution fusion | flops 202899456 | bytes 8650752 | tf_op jit(solution)/shard_map/iqmn,iqjnp->ijmp/dot_general | solution.py:68
  214.8 3.4 %copy.57 = bf16[48,4,64,64]{3,2,1,0:T(8,128)(2,1)S(1)} copy(bf16[48,4,64,64]{2,3,1,0:T(8,128)(2,1)} %fusion.1) | data formatting | bytes 3145728 | tf_op jit(solution)/shard_map/convert_element_type | solution.py:105
  218.2 3.2 %reshape.165 = bf16[48,4,4096]{2,1,0:T(4,128)(2,1)} reshape(bf16[48,4,64,64]{3,2,1,0:T(8,128)(2,1)S(1)} %copy.57) | data formatting | bytes 3145728 | tf_op jit(solution)/shard_map/convert_element_type | solution.py:105
  (54 shorter events, 4.9 us)
Async XLA Ops:
  6.5 185.3 %all-reduce.4.cloned.1.call-start = ((), (), s32[]{:S(2)}) async-start(), calls=%async_computation | async-start | bytes 6291456 | tf_op jit(solution)/shard_map/psum | solution.py:13
  6.5 68.3 %collective-permute-start.2 = (bf16[48,4,4096]{2,1,0:T(4,128)(2,1)}, bf16[48,4,4096]{2,1,0:T(4,128)(2,1)S(1)}, u32[]{:S(2)}, u32[]{:S(2)}) collective-permute-start(bf16[48,4,4096]{2,1,0:T(4,128)(2,1)} %param.3), channel_id=1, source_target_pairs={{1,0},{2,1},{3,2},{4,3},{5,4},{6,5},{7,6},{8,7},{9,8},{10,9},{11,1... | collective-permute-start | bytes 4718600 | tf_op jit(solution)/shard_map/ppermute | solution.py:19
  20.2 54.1 %collective-permute-start = (s32[48,4]{1,0:T(8,128)S(1)}, s32[48,4]{1,0:T(8,128)S(1)}, u32[]{:S(2)}, u32[]{:S(2)}) collective-permute-start(s32[48,4]{1,0:T(8,128)S(1)} %copy.37), channel_id=1, source_target_pairs={{1,0},{2,1},{3,2},{4,3},{5,4},{6,5},{7,6},{8,7},{9,8},{10,9},{11,1... | collective-permute-start | bytes 2312 | tf_op jit(solution)/shard_map/ppermute | solution.py:19
  22.8 49.9 %collective-permute-start.1 = (s32[48]{0:T(128)}, s32[48]{0:T(128)S(1)}, u32[]{:S(2)}, u32[]{:S(2)}) collective-permute-start(s32[48]{0:T(128)} %bitcast.53), channel_id=1, source_target_pairs={{1,0},{2,1},{3,2},{4,3},{5,4},{6,5},{7,6},{8,7},{9,8},{10,9},{11,1... | collective-permute-start | bytes 584 | tf_op jit(solution)/shard_map/ppermute | solution.py:19
  25.5 4.4 %copy-start = (s32[48,1]{0,1:T(1,128)S(1)}, s32[48,1]{0,1:T(1,128)}, u32[]{:S(2)}) copy-start(s32[48,1]{0,1:T(1,128)} %param.5) | copy-start | bytes 580
  25.5 4.4 %copy-start.3 = (s32[48,4]{0,1:T(4,128)S(1)}, s32[48,4]{0,1:T(4,128)}, u32[]{:S(2)}) copy-start(s32[48,4]{0,1:T(4,128)} %param.4) | copy-start | bytes 2308
  25.6 20.8 %copy-start.1 = (bf16[48,4,4096]{2,1,0:T(4,128)(2,1)S(1)}, bf16[48,4,4096]{2,1,0:T(4,128)(2,1)}, u32[]{:S(2)}) copy-start(bf16[48,4,4096]{2,1,0:T(4,128)(2,1)} %param.3) | copy-start | bytes 4718596
  198.5 9.8 %slice-start = ((s8[6291456]{0:T(1024)(128)(4,1)}), s8[2097152]{0:T(1024)(128)(4,1)S(1)}, s32[]{:S(2)}) async-start(s8[6291456]{0:T(1024)(128)(4,1)} %bitcast.56), calls=%async_computation.1 | async-start | bytes 4194304
  200.4 7.9 %slice-start.1 = ((s8[6291456]{0:T(1024)(128)(4,1)}), s8[4194304]{0:T(1024)(128)(4,1)S(1)}, s32[]{:S(2)}) async-start(s8[6291456]{0:T(1024)(128)(4,1)} %bitcast.56), calls=%async_computation.2 | async-start | bytes 8388608
  200.4 7.9 %copy-start.2 = (bf16[48,2,64,64,1]{3,2,1,0,4:T(8,128)(2,1)S(1)}, bf16[48,2,64,64,1]{3,2,1,0,4:T(8,128)(2,1)}, u32[]{:S(2)}) copy-start(bf16[48,2,64,64,1]{3,2,1,0,4:T(8,128)(2,1)} %reshape.161) | copy-start | bytes 2359300
Sparse Core Ops, SparseCore 0:
  30.1 161.6 all-reduce.3
where the time goes:
time: 229 us; the launch traced here: 228 us
  waiting for transfers between devices  94.2 us (41%)
  local copies, waits for them, and re-layouts  51 us (22%)
  matrix products  30.1 us (13%)
  starting transfers between devices  18.1 us (8%)
  between operations  13.7 us (6%)
  blocking collectives  12.7 us (6%)
  other arithmetic  8.37 us (4%)
    psum x1, waiting for transfers between devices, broadcast(): return lax.psum(block, axis)  94.2 us
    reshape x2, local copies, waits for them, and re-layouts, section_term(): right_sel = selected.reshape(strip_count, HS, slot_count, BLK, BLK)  20 us
    ppermute x3, starting transfers between devices, from_behind(): return lax.ppermute(block, axis, route)  18.1 us
    gather x2, local copies, waits for them, and re-layouts, section_term(): gathered = right_blocks[inner_rows]  14.6 us
    dot_general x2, matrix products, section_term(): jnp.einsum('iqmn,iqjnp->ijmp', left_blocks, right_sel, preferred_element_...  14.4 us
    psum x1, blocking collectives, broadcast(): return lax.psum(block, axis)  12.7 us
    dot_general x2, matrix products, section_term(): jnp.einsum('iqbj,iqbx->iqjx', matches.astype(jnp.bfloat16), gathered, pre...  11 us
    convert_element_type x2, local copies, waits for them, and re-layouts, local(): return accumulated.astype(jnp.bfloat16)  6.61 us
  transfers between devices with their start and end apart: 4, of which 1 were waited for; matrix products, arithmetic and copies ran while one was open for 26% of the time, Pallas kernels for 0%

commit v1 on v0

v1 whole, which is shorter than its diff:
```python
import functools

import jax
import jax.numpy as jnp
from jax import lax
from jax.experimental import pallas as pl
from jax.experimental.pallas import tpu as pltpu
from jax.sharding import PartitionSpec as P

HALF = 2
SUB = 32
LANES = 128
LEFT = 32


def prep_kernel(hA_ref, cols_ref, counts_ref, tile_ref, ga_ref, gb_ref, om_ref, flat, index):
    rows = tile_ref.shape[0]
    slots = tile_ref.shape[1]
    tiles = tile_ref.shape[2] // LANES
    first = hA_ref[0]
    lane = lax.broadcasted_iota(jnp.int32, (1, LANES), 1)
    ga_ref[rows:] = jnp.zeros((ga_ref.shape[0] - rows,) + ga_ref.shape[1:], ga_ref.dtype)
    gb_ref[rows:] = jnp.zeros((gb_ref.shape[0] - rows,) + gb_ref.shape[1:], gb_ref.dtype)
    index[...] = jnp.zeros(index.shape, index.dtype)

    def row(i, _):
        buf = lax.rem(i, 2)
        count = counts_ref[0, i]
        used = [jnp.int32(0), jnp.int32(0)]
        at = [jnp.int32(0)] * (2 * HALF)
        col = [jnp.int32(-1)] * (2 * HALF)
        out_row = jnp.full((1, LANES), -1, jnp.int32)
        for j in range(slots):
            c = cols_ref[j, i]
            live = j < count
            second = (c >= rows).astype(jnp.int32)
            side = jnp.where(second == first, 0, 1)
            for x in range(2):
                here = live & (side == x)
                for k in range(HALF):
                    take = here & (used[x] == k)
                    at[x * HALF + k] = jnp.where(take, j, at[x * HALF + k])
                    col[x * HALF + k] = jnp.where(take, c, col[x * HALF + k])
                used[x] = used[x] + here.astype(jnp.int32)
            out_row = jnp.where(
                (lane < 16) & ((lane & 3) == j), jnp.where(live, c + 1, -1), out_row
            )
        om_ref[pl.ds(i, 1), :] = out_row.astype(jnp.float32)
        idx_row = jnp.zeros((1, LANES), jnp.int32)
        for r in range(2 * HALF):
            inner = jnp.where(col[r] >= rows, col[r] - rows, col[r])
            idx_row = jnp.where((lane < 16) & ((lane >> 2) == r), col[r] + 1, idx_row)
            idx_row = jnp.where(lane == LEFT + r, jnp.where(col[r] < 0, 255, inner), idx_row)
        index[pl.ds(i, 1), :] = idx_row.astype(jnp.float32)
        v = tile_ref[i].astype(jnp.float32)
        for t in range(tiles):
            flat[buf, pl.ds(slots * t, slots), :] = v[:, t * LANES : (t + 1) * LANES]
        for r in range(2 * HALF):
            x = flat[buf, pl.ds(at[r], SUB, stride=slots), :].astype(ga_ref.dtype)
            dst = ga_ref if r < HALF else gb_ref
            dst[i, r % HALF] = x
        return 0

    lax.fori_loop(0, rows, row, 0)
    packed = index[...].astype(ga_ref.dtype)
    for dst in (ga_ref, gb_ref):
        for k in range(HALF):
            dst[rows, k] = packed[k * SUB : (k + 1) * SUB]


def prep(first, cols_t, counts_t, tile):
    rows, slots, size = tile.shape
    pad = rows + 2
    half = jax.ShapeDtypeStruct((pad, HALF, SUB, LANES), tile.dtype)
    smem = pl.BlockSpec(memory_space=pltpu.SMEM)
    vmem = pl.BlockSpec(memory_space=pltpu.VMEM)
    return pl.pallas_call(
        prep_kernel,
        out_shape=(half, half, jax.ShapeDtypeStruct((rows, LANES), jnp.float32)),
        in_specs=[smem, smem, smem, vmem],
        out_specs=(vmem, vmem, vmem),
        scratch_shapes=[
            pltpu.VMEM((2, slots * size // LANES, LANES), jnp.float32),
            pltpu.VMEM((HALF * SUB, LANES), jnp.float32),
        ],
        compiler_params=pltpu.CompilerParams(vmem_limit_bytes=24 << 20),
        name="prep",
    )(first, cols_t, counts_t, tile)


def multiply_kernel(
    sec_ref, om_ref, ga, gb, za, zb, hf, ho, out_ref, right, left, table, tsm, acc, wide, sems, tsem
):
    rows = out_ref.shape[0]
    slots = out_ref.shape[1]
    tiles = out_ref.shape[2] // LANES
    copies = [
        pltpu.make_async_copy(src, dst, sems.at[n])
        for n, (src, dst) in enumerate(
            (
                (ga, right.at[0]),
                (gb, right.at[1]),
                (za, right.at[2]),
                (zb, right.at[3]),
                (hf, left.at[0]),
                (ho, left.at[1]),
            )
        )
    ]
    for c in copies:
        c.start()
    sec = sec_ref[0]
    lane = lax.broadcasted_iota(jnp.int32, (rows, LANES), 1)
    low = lax.broadcasted_iota(jnp.int32, (2 * SUB, LANES), 1) < LANES // 2
    weight = jnp.zeros((rows, LANES), jnp.float32)
    for r in range(2 * HALF):
        weight = jnp.where((lane >> 2) == r, ((lane & 3) + 1).astype(jnp.float32) * 8.0**r, weight)
    weight = jnp.where(lane < 16, weight, 0.0)
    for c in copies:
        c.wait()
    found = jnp.zeros((rows, LANES), jnp.float32)
    total = jnp.zeros((rows, 1), jnp.float32)
    om = om_ref[...]
    for x in range(2):
        s = sec if x == 0 else 1 - sec
        rm = jnp.concatenate([right[2 * s, rows, k] for k in range(HALF)], 0)
        lm = jnp.concatenate([left[x, rows, k] for k in range(HALF)], 0)[:rows].astype(jnp.float32)
        for k in range(HALF):
            e = jnp.sum(jnp.where(lane == LEFT + 2 * s + k, lm, 0.0), axis=1, keepdims=True)
            pick = (lane[:, : HALF * SUB].astype(jnp.float32) == e).astype(rm.dtype)
            got = jnp.dot(pick, rm, preferred_element_type=jnp.float32)
            code = jnp.sum(jnp.where(got == om, weight, 0.0), axis=1, keepdims=True)
            found = jnp.where(lane == x * HALF + k, code, found)
            found = jnp.where(lane == 8 + x * HALF + k, e, found)
            total = total + code
    found = jnp.where(lane == 4, total, found)
    table[...] = found.astype(jnp.int32)
    put = pltpu.make_async_copy(table, tsm, tsem)
    put.start()
    put.wait()

    def row(i, _):
        any_match = tsm[i, 4]

        @pl.when(any_match == 0)
        def _():
            out_ref[i] = jnp.zeros(out_ref.shape[1:], out_ref.dtype)

        @pl.when(any_match != 0)
        def _():
            acc[...] = jnp.zeros(acc.shape, acc.dtype)
            for x in range(2):
                s = sec if x == 0 else 1 - sec
                for k in range(HALF):
                    code = tsm[i, x * HALF + k]

                    @pl.when(code != 0)
                    def _(x=x, k=k, s=s, code=code):
                        e = tsm[i, 8 + x * HALF + k]

                        def slot(r, _):
                            j = lax.shift_right_logical(code, 3 * r) & 7

                            @pl.when(j != 0)
                            def _():
                                b = right[2 * s + lax.shift_right_logical(r, 1), e, r & 1]
                                b = b.astype(jnp.float32)
                                wide[pl.ds(0, SUB, stride=2), :] = b
                                wide[pl.ds(1, SUB, stride=2), :] = pltpu.roll(b, LANES // 2, 1)
                                w = wide[...]
                                diag = jnp.concatenate(
                                    [
                                        jnp.where(low, w, 0.0),
                                        jnp.where(low, 0.0, pltpu.roll(w, LANES // 2, 1)),
                                    ],
                                    0,
                                ).astype(left.dtype)
                                got = jnp.dot(
                                    left[x, i, k], diag, preferred_element_type=jnp.float32
                                )
                                at = pl.ds(j - 1, SUB, stride=slots)
                                acc[at, :] = acc[at, :] + got

                            return 0

                        lax.fori_loop(0, 2 * HALF, slot, 0)

            for t in range(tiles):
                out_ref[i, :, t * LANES : (t + 1) * LANES] = acc[
                    pl.ds(slots * t, slots), :
                ].astype(out_ref.dtype)

        return 0

    lax.fori_loop(0, rows, row, 0)


def multiply(sec, om, ga, gb, za, zb, hf, ho, slots):
    rows = om.shape[0]
    size = 2 * SUB * SUB * 2
    hbm = pl.BlockSpec(memory_space=pl.ANY)
    vmem = pl.BlockSpec(memory_space=pltpu.VMEM)
    return pl.pallas_call(
        multiply_kernel,
        out_shape=jax.ShapeDtypeStruct((rows, slots, size), ga.dtype),
        in_specs=[pl.BlockSpec(memory_space=pltpu.SMEM), vmem] + [hbm] * 6,
        out_specs=vmem,
        scratch_shapes=[
            pltpu.VMEM((4,) + ga.shape, ga.dtype),
            pltpu.VMEM((2,) + ga.shape, ga.dtype),
            pltpu.VMEM((rows, LANES), jnp.int32),
            pltpu.SMEM((rows, LANES), jnp.int32),
            pltpu.VMEM((slots * size // LANES, LANES), jnp.float32),
            pltpu.VMEM((2 * SUB, LANES), jnp.float32),
            pltpu.SemaphoreType.DMA((6,)),
            pltpu.SemaphoreType.DMA,
        ],
        compiler_params=pltpu.CompilerParams(vmem_limit_bytes=32 << 20),
        name="multiply",
    )(sec, om, ga, gb, za, zb, hf, ho)


def local(blocks, columns, counts, n_row, n_col):
    slots = columns.shape[1]
    p = lax.axis_index("col")
    q = lax.axis_index("row")
    k = p // 2
    even = p % 2 == 0
    root_a = k
    root_b = jnp.where(even, k ^ 1, (k + 1) % n_row)
    in_a = (q & 1) == (root_a & 1)
    root = jnp.where(in_a, root_a, root_b)
    role = (((q >> 1) & 3) - ((root >> 1) & 3)) % 4

    ga, gb, om = prep((p % 2).reshape(1).astype(jnp.int32), columns.T, counts.T, blocks)

    to_a, to_b, to_core = [], [], []
    for c in range(n_col):
        owner_a = c // 2
        owner_b = owner_a if c % 2 == 0 else (owner_a + 1) % n_row
        tree_b = owner_b ^ 1 if c % 2 == 0 else owner_b
        to_a.append((owner_a * n_col + c, (owner_a ^ 8) * n_col + c))
        to_b.append((owner_b * n_col + c, (tree_b ^ 8) * n_col + c))
        if owner_b != tree_b:
            to_core.append((owner_b * n_col + c, tree_b * n_col + c))
    both = ("row", "col")
    from_next = [((i + 1) % n_col, i) for i in range(n_col)]

    def along_y(v, d):
        route = [(i, (i & ~6) | ((((i >> 1) & 3) + d) % 4) << 1) for i in range(n_row)]
        return lax.ppermute(v, "row", route)

    got_a = lax.ppermute(ga, both, to_a)
    got_b = lax.ppermute(gb, both, to_b)
    got_core = lax.ppermute(gb, both, to_core)
    za = lax.ppermute(ga, "col", from_next)
    got_a, got_b, got_core, za = lax.optimization_barrier((got_a, got_b, got_core, za))
    start = jnp.where(q == root_a, ga, jnp.where((q == root_b) & ~even, gb, got_a + got_b + got_core))
    mid = start.shape[0] // 2
    a, b = start[:mid], start[mid:]
    top = role == 0
    up = along_y(a, 1)
    down = along_y(b, -1)
    up, down = lax.optimization_barrier((up, down))
    up2 = along_y(jnp.where(top, b, up), 1)
    down2 = along_y(jnp.where(top, a, down), -1)
    zb = lax.ppermute(gb, "col", from_next)
    up2, down2, zb = lax.optimization_barrier((up2, down2, zb))
    half_a = jnp.where(top, a, jnp.where(role == 1, up, jnp.where(role == 3, down2, up2)))
    half_b = jnp.where(top, b, jnp.where(role == 1, up2, jnp.where(role == 3, down, down2)))
    mine = jnp.concatenate([half_a, half_b], 0)
    other = lax.ppermute(mine, "row", [(i, i ^ 1) for i in range(n_row)])
    sec = jnp.where(in_a, 0, 1).reshape(1).astype(jnp.int32)
    return multiply(sec, om, ga, gb, za, zb, mine, other, slots)


def solution(mesh):
    step = functools.partial(local, n_row=mesh.shape["row"], n_col=mesh.shape["col"])
    return jax.shard_map(
        step,
        mesh=mesh,
        in_specs=(P("col", "row", None), P("col", "row"), P("col", "row")),
        out_specs=P("col", "row", None),
        check_vma=False,
    )
```

time: 229 us -> 103 us (0.45)
  the two profiles are of different devices: /device:TPU:1 before, /device:TPU:28 now
where the time goes in v1:
time: 103 us
  starting transfers between devices  40.6 us (39%)
  waiting for transfers between devices  31.7 us (31%)
  Pallas kernels  19.6 us (19%)
  other arithmetic  5.63 us (5%)
  local copies, waits for them, and re-layouts  4.92 us (5%)
    ppermute x1, waiting for transfers between devices, local(): za = lax.ppermute(ga, 'col', from_next)  17.3 us
    pallas_call x1, Pallas kernels, multiply(): pl.pallas_call(multiply_kernel, out_shape=jax.ShapeDtypeStruct((rows, slo...  16.1 us
    ppermute x1, starting transfers between devices, local(): za = lax.ppermute(ga, 'col', from_next)  12 us
    ppermute x4, starting transfers between devices, along_y(): return lax.ppermute(v, 'row', route)  11.7 us
    ppermute x1, starting transfers between devices, local(): zb = lax.ppermute(gb, 'col', from_next)  11.1 us
    ppermute x4, waiting for transfers between devices, along_y(): return lax.ppermute(v, 'row', route)  6.79 us
    ppermute x1, waiting for transfers between devices, local(): zb = lax.ppermute(gb, 'col', from_next)  5.18 us
    unnamed x12, local copies, waits for them, and re-layouts  3.9 us
  transfers between devices with their start and end apart: 10, of which 6 were waited for; matrix products, arithmetic and copies ran while one was open for 2% of the time, Pallas kernels for 0%

profile of v1, /device:TPU:28, one launch (start us, length us, event | category | flops | bytes accessed | tf_op | source)
XLA Modules:
  0.0 102.7 jit_solution(4969045656797319234)
XLA Ops:
  0.0 1.4 %copy-done = bf16[48,4,4096]{2,1,0:T(4,128)(2,1)S(1)} copy-done((bf16[48,4,4096]{2,1,0:T(4,128)(2,1)S(1)}, bf16[48,4,4096]{2,1,0:T(4,128)(2,1)}, u32[]{:S(2)}) %copy-start) | copy-done | bytes 1572888
  2.7 3.6 %prep.1 = (bf16[50,2,32,128]{3,2,1,0:T(8,128)(2,1)S(1)}, bf16[50,2,32,128]{3,2,1,0:T(8,128)(2,1)S(1)}, f32[48,128]{1,0:T(8,128)S(1)}) custom-call(s32[1]{0:T(128)} %bitcast.1.hA_ref, s32[4,48]{1,0:T(4,128)S(1)} %bitcast.4, s32[1,48]{1,0:T(1,128)S(1)} %bitcast.5, bf16[48,4,4096]{2,1,0:T(4,128)(2,1)S(1)} %copy-done), custom_call_target="tpu_custom_call" | custom-call | tf_op jit(solution)/shard_map/prep/pallas_call | solution.py:77
  6.3 0.7 collective-permute-start
  7.0 1.6 %collective-permute-start.1 = (bf16[50,2,32,128]{3,2,1,0:T(8,128)(2,1)S(1)}, bf16[50,2,32,128]{3,2,1,0:T(8,128)(2,1)}, u32[]{:S(2)}, u32[]{:S(2)}) collective-permute-start(bf16[50,2,32,128]{3,2,1,0:T(8,128)(2,1)S(1)} %get-tuple-element.19.gb), channel_id=1, source_target_pairs={{0,288},{33,289},{34,258},{67,323},{68,356},{101,357},{102,326},{1... | collective-permute-start | bytes 2457608 | tf_op jit(solution)/shard_map/ppermute | solution.py:254
  8.6 1.5 %collective-permute-start.2 = (bf16[50,2,32,128]{3,2,1,0:T(8,128)(2,1)S(1)}, bf16[50,2,32,128]{3,2,1,0:T(8,128)(2,1)}, u32[]{:S(2)}, u32[]{:S(2)}) collective-permute-start(bf16[50,2,32,128]{3,2,1,0:T(8,128)(2,1)S(1)} %get-tuple-element.19.gb), channel_id=1, source_target_pairs={{0,32},{34,2},{68,100},{102,70},{136,168},{170,138},{204,236},{238... | collective-permute-start | bytes 2457608 | tf_op jit(solution)/shard_map/ppermute | solution.py:255
  10.2 12.0 %collective-permute-start.3 = (bf16[50,2,32,128]{3,2,1,0:T(8,128)(2,1)S(1)}, bf16[50,2,32,128]{3,2,1,0:T(8,128)(2,1)S(1)}, u32[]{:S(2)}, u32[]{:S(2)}) collective-permute-start(bf16[50,2,32,128]{3,2,1,0:T(8,128)(2,1)S(1)} %get-tuple-element.18.ga), channel_id=1, source_target_pairs={{1,0},{2,1},{3,2},{4,3},{5,4},{6,5},{7,6},{8,7},{9,8},{10,9},{11,1... | collective-permute-start | bytes 2457608 | tf_op jit(solution)/shard_map/ppermute | solution.py:256
  22.3 17.3 %collective-permute-done.3.za = bf16[50,2,32,128]{3,2,1,0:T(8,128)(2,1)S(1)} collective-permute-done((bf16[50,2,32,128]{3,2,1,0:T(8,128)(2,1)S(1)}, bf16[50,2,32,128]{3,2,1,0:T(8,128)(2,1)S(1)}, u32[]{:S(2)}, u32[]{:S(2)}) %collective-permute-start.3) | collective-permute-done | bytes 819232 | tf_op jit(solution)/shard_map/ppermute | solution.py:256
  39.6 1.6 %select_select_fusion = bf16[50,2,32,128]{3,2,1,0:T(8,128)(2,1)S(1)} fusion(bf16[50,2,32,128]{3,2,1,0:T(8,128)(2,1)S(1)} %get-tuple-element.18.ga, bf16[50,2,32,128]{3,2,1,0:T(8,128)(2,1)S(1)} %get-tuple-element.19.gb, bf16[50,2,32,128]{3,2,1,0:T(8,128)(2,1)} %collective-permute-done.2, bf16[50,2,32,128]{3,2,1,0:T(8,128)(2,1)S(1)} %collective-permute-done, ...), kind=kLoop, calls=%fused_computation.1 | loop fusion | flops 1638400 | bytes 4915202 | tf_op jit(solution)/shard_map/jit(_where)/select_n | solution.py:258
  41.2 1.0 fusion
  42.2 2.3 %collective-permute-start.4 = (bf16[25,2,32,128]{3,2,1,0:T(8,128)(2,1)}, bf16[25,2,32,128]{3,2,1,0:T(8,128)(2,1)}, u32[]{:S(2)}, u32[]{:S(2)}) collective-permute-start(bf16[25,2,32,128]{3,2,1,0:T(8,128)(2,1)} %get-tuple-element.34), channel_id=1, source_target_pairs={{0,64},{32,96},{64,128},{96,160},{128,192},{160,224},{192,0},{224,... | collective-permute-start | bytes 1228808 | tf_op jit(solution)/shard_map/ppermute | solution.py:251
  44.5 3.5 %collective-permute-start.5 = (bf16[25,2,32,128]{3,2,1,0:T(8,128)(2,1)}, bf16[25,2,32,128]{3,2,1,0:T(8,128)(2,1)}, u32[]{:S(2)}, u32[]{:S(2)}) collective-permute-start(bf16[25,2,32,128]{3,2,1,0:T(8,128)(2,1)} %get-tuple-element.33), channel_id=1, source_target_pairs={{0,192},{32,224},{64,0},{96,32},{128,64},{160,96},{192,128},{224,1... | collective-permute-start | bytes 1228808 | tf_op jit(solution)/shard_map/ppermute | solution.py:251
  48.0 11.1 %collective-permute-start.8 = (bf16[50,2,32,128]{3,2,1,0:T(8,128)(2,1)S(1)}, bf16[50,2,32,128]{3,2,1,0:T(8,128)(2,1)S(1)}, u32[]{:S(2)}, u32[]{:S(2)}) collective-permute-start(bf16[50,2,32,128]{3,2,1,0:T(8,128)(2,1)S(1)} %get-tuple-element.19.gb), channel_id=1, source_target_pairs={{1,0},{2,1},{3,2},{4,3},{5,4},{6,5},{7,6},{8,7},{9,8},{10,9},{11,1... | collective-permute-start | bytes 2457608 | tf_op jit(solution)/shard_map/ppermute | solution.py:267
  59.2 1.0 collective-permute-done.5
  60.2 2.4 %broadcast_select_fusion = (bf16[25,2,32,128]{3,2,1,0:T(8,128)(2,1)}, bf16[25,2,32,128]{3,2,1,0:T(8,128)(2,1)}) fusion(bf16[25,2,32,128]{3,2,1,0:T(8,128)(2,1)} %collective-permute-done.5, pred[]{:T(512)S(6)} %eq.30, bf16[50,2,32,128]{3,2,1,0:T(8,128)(2,1)} %copy-done.5, bf16[25,2,32,128]{3,2,1,0:T(8,128)(2,1)} %collective-permute-done.4), kind=kLoop, calls=%fused_computation.4 | loop fusion | flops 409600 | bytes 2457601 | tf_op jit(solution)/shard_map/jit(_where)/select_n | solution.py:266
  62.6 3.9 %collective-permute-start.6 = (bf16[25,2,32,128]{3,2,1,0:T(8,128)(2,1)}, bf16[25,2,32,128]{3,2,1,0:T(8,128)(2,1)}, u32[]{:S(2)}, u32[]{:S(2)}) collective-permute-start(bf16[25,2,32,128]{3,2,1,0:T(8,128)(2,1)} %get-tuple-element.32), channel_id=1, source_target_pairs={{0,64},{32,96},{64,128},{96,160},{128,192},{160,224},{192,0},{224,... | collective-permute-start | bytes 1228808 | tf_op jit(solution)/shard_map/ppermute | solution.py:251
  66.5 1.9 %collective-permute-start.7 = (bf16[25,2,32,128]{3,2,1,0:T(8,128)(2,1)}, bf16[25,2,32,128]{3,2,1,0:T(8,128)(2,1)}, u32[]{:S(2)}, u32[]{:S(2)}) collective-permute-start(bf16[25,2,32,128]{3,2,1,0:T(8,128)(2,1)} %get-tuple-element.31), channel_id=1, source_target_pairs={{0,192},{32,224},{64,0},{96,32},{128,64},{160,96},{192,128},{224,1... | collective-permute-start | bytes 1228808 | tf_op jit(solution)/shard_map/ppermute | solution.py:251
  68.4 5.2 %collective-permute-done.8.zb = bf16[50,2,32,128]{3,2,1,0:T(8,128)(2,1)S(1)} collective-permute-done((bf16[50,2,32,128]{3,2,1,0:T(8,128)(2,1)S(1)}, bf16[50,2,32,128]{3,2,1,0:T(8,128)(2,1)S(1)}, u32[]{:S(2)}, u32[]{:S(2)}) %collective-permute-start.8) | collective-permute-done | bytes 819232 | tf_op jit(solution)/shard_map/ppermute | solution.py:267
  73.6 2.6 %collective-permute-done.6 = bf16[25,2,32,128]{3,2,1,0:T(8,128)(2,1)} collective-permute-done((bf16[25,2,32,128]{3,2,1,0:T(8,128)(2,1)}, bf16[25,2,32,128]{3,2,1,0:T(8,128)(2,1)}, u32[]{:S(2)}, u32[]{:S(2)}) %collective-permute-start.6) | collective-permute-done | bytes 409632 | tf_op jit(solution)/shard_map/ppermute | solution.py:251
  76.3 3.1 %collective-permute-done.7 = bf16[25,2,32,128]{3,2,1,0:T(8,128)(2,1)} collective-permute-done((bf16[25,2,32,128]{3,2,1,0:T(8,128)(2,1)}, bf16[25,2,32,128]{3,2,1,0:T(8,128)(2,1)}, u32[]{:S(2)}, u32[]{:S(2)}) %collective-permute-start.7) | collective-permute-done | bytes 409632 | tf_op jit(solution)/shard_map/ppermute | solution.py:251
  79.4 1.6 %select_select_fusion.2 = (bf16[25,2,32,128]{3,2,1,0:T(8,128)(2,1)S(1)}, bf16[25,2,32,128]{3,2,1,0:T(8,128)(2,1)S(1)}) fusion(bf16[25,2,32,128]{3,2,1,0:T(8,128)(2,1)} %collective-permute-done.4, bf16[25,2,32,128]{3,2,1,0:T(8,128)(2,1)} %collective-permute-done.7, bf16[25,2,32,128]{3,2,1,0:T(8,128)(2,1)} %collective-permute-done.6, pred[]{:T(512)S(6)} %eq.34, ...), kind=kLoop, calls=%fused_computation.3 | loop fusion | flops 1228800 | bytes 3276803 | tf_op jit(solution)/shard_map/jit(_where)/select_n | solution.py:269
  81.1 1.9 %collective-permute-start.9 = (bf16[50,2,32,128]{3,2,1,0:T(8,128)(2,1)S(1)}, bf16[50,2,32,128]{3,2,1,0:T(8,128)(2,1)}, u32[]{:S(2)}, u32[]{:S(2)}) collective-permute-start(bf16[50,2,32,128]{3,2,1,0:T(8,128)(2,1)S(1)} %pad_maximum_fusion.hf), channel_id=1, source_target_pairs={{0,32},{32,0},{64,96},{96,64},{128,160},{160,128},{192,224},{224,1... | collective-permute-start | bytes 2457608 | tf_op jit(solution)/shard_map/ppermute | solution.py:272
  83.1 2.4 %collective-permute-done.9.ho = bf16[50,2,32,128]{3,2,1,0:T(8,128)(2,1)} collective-permute-done((bf16[50,2,32,128]{3,2,1,0:T(8,128)(2,1)S(1)}, bf16[50,2,32,128]{3,2,1,0:T(8,128)(2,1)}, u32[]{:S(2)}, u32[]{:S(2)}) %collective-permute-start.9) | collective-permute-done | bytes 819232 | tf_op jit(solution)/shard_map/ppermute | solution.py:272
  85.5 1.1 %copy-done.2 = bf16[50,2,32,128]{3,2,1,0:T(8,128)(2,1)S(1)} copy-done((bf16[50,2,32,128]{3,2,1,0:T(8,128)(2,1)S(1)}, bf16[50,2,32,128]{3,2,1,0:T(8,128)(2,1)}, u32[]{:S(2)}) %copy-start.2) | copy-done | bytes 819224
  86.6 16.1 %multiply.1 = bf16[48,4,4096]{2,1,0:T(4,128)(2,1)} custom-call(s32[1]{0:T(128)} %bitcast.sec_ref, f32[48,128]{1,0:T(8,128)S(1)} %get-tuple-element.17.om_ref, bf16[50,2,32,128]{3,2,1,0:T(8,128)(2,1)S(1)} %get-tuple-element.18.ga, bf16[50,2,32,128]{3,2,1,0:T(8,128)(2,1)S(1)} %get-tuple-element.19.gb, bf16[50,2,32,128]{3,2,1,0:T(8,128)(2,1)S(1)} %collective-permute-done.3.za, ...), custom_call_target="tpu_custom_call" | custom-call | tf_op jit(solution)/shard_map/multiply/pallas_call | solution.py:203
  (15 shorter events, 1.4 us)
Async XLA Ops:
  0.0 1.4 %copy-start = (bf16[48,4,4096]{2,1,0:T(4,128)(2,1)S(1)}, bf16[48,4,4096]{2,1,0:T(4,128)(2,1)}, u32[]{:S(2)}) copy-start(bf16[48,4,4096]{2,1,0:T(4,128)(2,1)} %tile_ref.1) | copy-start | bytes 4718596
  1.4 0.7 copy-start.3
  2.1 0.7 copy-start.4
  6.3 16.0 %collective-permute-start = (bf16[50,2,32,128]{3,2,1,0:T(8,128)(2,1)S(1)}, bf16[50,2,32,128]{3,2,1,0:T(8,128)(2,1)S(1)}, u32[]{:S(2)}, u32[]{:S(2)}) collective-permute-start(bf16[50,2,32,128]{3,2,1,0:T(8,128)(2,1)S(1)} %get-tuple-element.18.ga), channel_id=1, source_target_pairs={{0,256},{1,257},{34,290},{35,291},{68,324},{69,325},{102,358},{103... | collective-permute-start | bytes 2457608 | tf_op jit(solution)/shard_map/ppermute | solution.py:253
  7.0 15.2 %collective-permute-start.1 = (bf16[50,2,32,128]{3,2,1,0:T(8,128)(2,1)S(1)}, bf16[50,2,32,128]{3,2,1,0:T(8,128)(2,1)}, u32[]{:S(2)}, u32[]{:S(2)}) collective-permute-start(bf16[50,2,32,128]{3,2,1,0:T(8,128)(2,1)S(1)} %get-tuple-element.19.gb), channel_id=1, source_target_pairs={{0,288},{33,289},{34,258},{67,323},{68,356},{101,357},{102,326},{1... | collective-permute-start | bytes 2457608 | tf_op jit(solution)/shard_map/ppermute | solution.py:254
  8.6 13.7 %collective-permute-start.2 = (bf16[50,2,32,128]{3,2,1,0:T(8,128)(2,1)S(1)}, bf16[50,2,32,128]{3,2,1,0:T(8,128)(2,1)}, u32[]{:S(2)}, u32[]{:S(2)}) collective-permute-start(bf16[50,2,32,128]{3,2,1,0:T(8,128)(2,1)S(1)} %get-tuple-element.19.gb), channel_id=1, source_target_pairs={{0,32},{34,2},{68,100},{102,70},{136,168},{170,138},{204,236},{238... | collective-permute-start | bytes 2457608 | tf_op jit(solution)/shard_map/ppermute | solution.py:255
  10.2 29.4 %collective-permute-start.3 = (bf16[50,2,32,128]{3,2,1,0:T(8,128)(2,1)S(1)}, bf16[50,2,32,128]{3,2,1,0:T(8,128)(2,1)S(1)}, u32[]{:S(2)}, u32[]{:S(2)}) collective-permute-start(bf16[50,2,32,128]{3,2,1,0:T(8,128)(2,1)S(1)} %get-tuple-element.18.ga), channel_id=1, source_target_pairs={{1,0},{2,1},{3,2},{4,3},{5,4},{6,5},{7,6},{8,7},{9,8},{10,9},{11,1... | collective-permute-start | bytes 2457608 | tf_op jit(solution)/shard_map/ppermute | solution.py:256
  41.1 3.3 %copy-start.5 = (bf16[50,2,32,128]{3,2,1,0:T(8,128)(2,1)}, bf16[50,2,32,128]{3,2,1,0:T(8,128)(2,1)S(1)}, u32[]{:S(2)}) copy-start(bf16[50,2,32,128]{3,2,1,0:T(8,128)(2,1)S(1)} %select_select_fusion) | copy-start | bytes 2457604
  42.2 17.0 %collective-permute-start.4 = (bf16[25,2,32,128]{3,2,1,0:T(8,128)(2,1)}, bf16[25,2,32,128]{3,2,1,0:T(8,128)(2,1)}, u32[]{:S(2)}, u32[]{:S(2)}) collective-permute-start(bf16[25,2,32,128]{3,2,1,0:T(8,128)(2,1)} %get-tuple-element.34), channel_id=1, source_target_pairs={{0,64},{32,96},{64,128},{96,160},{128,192},{160,224},{192,0},{224,... | collective-permute-start | bytes 1228808 | tf_op jit(solution)/shard_map/ppermute | solution.py:251
  44.5 15.7 %collective-permute-start.5 = (bf16[25,2,32,128]{3,2,1,0:T(8,128)(2,1)}, bf16[25,2,32,128]{3,2,1,0:T(8,128)(2,1)}, u32[]{:S(2)}, u32[]{:S(2)}) collective-permute-start(bf16[25,2,32,128]{3,2,1,0:T(8,128)(2,1)} %get-tuple-element.33), channel_id=1, source_target_pairs={{0,192},{32,224},{64,0},{96,32},{128,64},{160,96},{192,128},{224,1... | collective-permute-start | bytes 1228808 | tf_op jit(solution)/shard_map/ppermute | solution.py:251
  48.0 25.6 %collective-permute-start.8 = (bf16[50,2,32,128]{3,2,1,0:T(8,128)(2,1)S(1)}, bf16[50,2,32,128]{3,2,1,0:T(8,128)(2,1)S(1)}, u32[]{:S(2)}, u32[]{:S(2)}) collective-permute-start(bf16[50,2,32,128]{3,2,1,0:T(8,128)(2,1)S(1)} %get-tuple-element.19.gb), channel_id=1, source_target_pairs={{1,0},{2,1},{3,2},{4,3},{5,4},{6,5},{7,6},{8,7},{9,8},{10,9},{11,1... | collective-permute-start | bytes 2457608 | tf_op jit(solution)/shard_map/ppermute | solution.py:267
  62.6 13.7 %collective-permute-start.6 = (bf16[25,2,32,128]{3,2,1,0:T(8,128)(2,1)}, bf16[25,2,32,128]{3,2,1,0:T(8,128)(2,1)}, u32[]{:S(2)}, u32[]{:S(2)}) collective-permute-start(bf16[25,2,32,128]{3,2,1,0:T(8,128)(2,1)} %get-tuple-element.32), channel_id=1, source_target_pairs={{0,64},{32,96},{64,128},{96,160},{128,192},{160,224},{192,0},{224,... | collective-permute-start | bytes 1228808 | tf_op jit(solution)/shard_map/ppermute | solution.py:251
  66.5 12.9 %collective-permute-start.7 = (bf16[25,2,32,128]{3,2,1,0:T(8,128)(2,1)}, bf16[25,2,32,128]{3,2,1,0:T(8,128)(2,1)}, u32[]{:S(2)}, u32[]{:S(2)}) collective-permute-start(bf16[25,2,32,128]{3,2,1,0:T(8,128)(2,1)} %get-tuple-element.31), channel_id=1, source_target_pairs={{0,192},{32,224},{64,0},{96,32},{128,64},{160,96},{192,128},{224,1... | collective-permute-start | bytes 1228808 | tf_op jit(solution)/shard_map/ppermute | solution.py:251
  73.6 7.4 %copy-start.1 = (bf16[50,2,32,128]{3,2,1,0:T(8,128)(2,1)}, bf16[50,2,32,128]{3,2,1,0:T(8,128)(2,1)S(1)}, u32[]{:S(2)}) copy-start(bf16[50,2,32,128]{3,2,1,0:T(8,128)(2,1)S(1)} %collective-permute-done.8.zb) | copy-start | bytes 2457604
  81.1 4.4 %collective-permute-start.9 = (bf16[50,2,32,128]{3,2,1,0:T(8,128)(2,1)S(1)}, bf16[50,2,32,128]{3,2,1,0:T(8,128)(2,1)}, u32[]{:S(2)}, u32[]{:S(2)}) collective-permute-start(bf16[50,2,32,128]{3,2,1,0:T(8,128)(2,1)S(1)} %pad_maximum_fusion.hf), channel_id=1, source_target_pairs={{0,32},{32,0},{64,96},{96,64},{128,160},{160,128},{192,224},{224,1... | collective-permute-start | bytes 2457608 | tf_op jit(solution)/shard_map/ppermute | solution.py:272
  85.5 1.1 %copy-start.2 = (bf16[50,2,32,128]{3,2,1,0:T(8,128)(2,1)S(1)}, bf16[50,2,32,128]{3,2,1,0:T(8,128)(2,1)}, u32[]{:S(2)}) copy-start(bf16[50,2,32,128]{3,2,1,0:T(8,128)(2,1)} %copy-done.1) | copy-start | bytes 2457604

commit v2 on v1

v2 whole, which is shorter than its diff:
```python
import functools

import jax
import jax.numpy as jnp
from jax import lax
from jax.experimental import pallas as pl
from jax.experimental.pallas import tpu as pltpu
from jax.sharding import PartitionSpec as P

HALF = 2
SUB = 32
LANES = 128
AHEAD = 4
FIRST, WHICH, ROLE, HEAD, LAST, SECTION = range(6)
CROSS = 35
LEFT = 32
VMEM = pl.BlockSpec(memory_space=pltpu.VMEM)
SMEM = pl.BlockSpec(memory_space=pltpu.SMEM)


def prep_kernel(flags, table, tile, g, om_ref, flat, index):
    rows, slots, size = tile.shape
    tiles = size // LANES
    first = flags[FIRST]
    lane = lax.broadcasted_iota(jnp.int32, (1, LANES), 1)
    g[:, rows:] = jnp.zeros((2, g.shape[1] - rows) + g.shape[2:], g.dtype)
    index[...] = jnp.zeros(index.shape, index.dtype)

    def row(i, _):
        buf = lax.rem(i, 2)
        count = table[slots, i]
        used = [jnp.int32(0), jnp.int32(0)]
        at = [jnp.int32(0)] * (2 * HALF)
        col = [jnp.int32(-1)] * (2 * HALF)
        out_row = jnp.full((1, LANES), -1, jnp.int32)
        for j in range(slots):
            c = table[j, i]
            live = j < count
            second = (c >= rows).astype(jnp.int32)
            side = jnp.where(second == first, 0, 1)
            for x in range(2):
                here = live & (side == x)
                for k in range(HALF):
                    take = here & (used[x] == k)
                    at[x * HALF + k] = jnp.where(take, j, at[x * HALF + k])
                    col[x * HALF + k] = jnp.where(take, c, col[x * HALF + k])
                used[x] = used[x] + here.astype(jnp.int32)
            out_row = jnp.where(
                (lane < 16) & ((lane & 3) == j), jnp.where(live, c + 1, -1), out_row
            )
        om_ref[pl.ds(i, 1), :] = out_row.astype(jnp.float32)
        idx_row = jnp.zeros((1, LANES), jnp.int32)
        for r in range(2 * HALF):
            inner = jnp.where(col[r] >= rows, col[r] - rows, col[r])
            idx_row = jnp.where((lane < 16) & ((lane >> 2) == r), col[r] + 1, idx_row)
            idx_row = jnp.where(lane == LEFT + r, jnp.where(col[r] < 0, 255, inner), idx_row)
        index[pl.ds(i, 1), :] = idx_row.astype(jnp.float32)
        v = tile[i].astype(jnp.float32)
        for t in range(tiles):
            flat[buf, pl.ds(slots * t, slots), :] = v[:, t * LANES : (t + 1) * LANES]
        for r in range(2 * HALF):
            x = flat[buf, pl.ds(at[r], SUB, stride=slots), :].astype(g.dtype)
            g[r // HALF, i, r % HALF] = x
        return 0

    lax.fori_loop(0, rows, row, 0)
    packed = index[...].astype(g.dtype)
    for x in range(2):
        for k in range(HALF):
            g[x, rows, k] = packed[k * SUB : (k + 1) * SUB]


def prep(flags, table, tile):
    rows, slots, size = tile.shape
    return pl.pallas_call(
        prep_kernel,
        out_shape=(
            jax.ShapeDtypeStruct((2, rows + 2, HALF, SUB, LANES), tile.dtype),
            jax.ShapeDtypeStruct((rows, LANES), jnp.float32),
        ),
        in_specs=[SMEM, SMEM, VMEM],
        out_specs=(VMEM, VMEM),
        scratch_shapes=[
            pltpu.VMEM((2, slots * size // LANES, LANES), jnp.float32),
            pltpu.VMEM((HALF * SUB, LANES), jnp.float32),
        ],
        compiler_params=pltpu.CompilerParams(vmem_limit_bytes=12 << 20),
        name="prep",
    )(flags, table, tile)


def pick_kernel(flags, *refs):
    *sources, tile, a, b, whole, cross = refs
    mid = a.shape[0]
    for n, src in enumerate(sources):

        @pl.when(flags[WHICH] == n)
        def _(src=src):
            a[...] = src[:mid]
            b[...] = src[mid:]

    @pl.when(flags[HEAD] != 0)
    def _():
        rest = tile.shape[1] - CROSS
        whole[: tile.shape[1]] = tile[0]
        whole[tile.shape[1] :] = tile[1, :rest]
        cross[...] = tile[1, rest:]


def pick(flags, tile, *sources):
    shape = tile.shape[1:]
    piece = lambda n: jax.ShapeDtypeStruct((n,) + shape[1:], tile.dtype)
    return pl.pallas_call(
        pick_kernel,
        out_shape=(
            piece(shape[0] // 2),
            piece(shape[0] // 2),
            piece(2 * shape[0] - CROSS),
            piece(CROSS),
        ),
        in_specs=[SMEM] + [VMEM] * (len(sources) + 1),
        out_specs=(VMEM,) * 4,
        compiler_params=pltpu.CompilerParams(vmem_limit_bytes=4 << 20),
        name="pick",
    )(flags, *sources, tile)


def turn_kernel(flags, a, b, up, down, c, d):
    role = flags[ROLE]

    @pl.when(role == 0)
    def _():
        c[...] = b[...]
        d[...] = a[...]

    @pl.when(role == 1)
    def _():
        c[...] = up[...]

    @pl.when(role == 3)
    def _():
        d[...] = down[...]


def turn(flags, *pieces):
    piece = jax.ShapeDtypeStruct(pieces[0].shape, pieces[0].dtype)
    return pl.pallas_call(
        turn_kernel,
        out_shape=(piece, piece),
        in_specs=[SMEM] + [VMEM] * len(pieces),
        out_specs=(VMEM, VMEM),
        compiler_params=pltpu.CompilerParams(vmem_limit_bytes=4 << 20),
        name="turn",
    )(flags, *pieces)


def join_kernel(flags, *refs):
    *pieces, wrap, cross, behind, out, right = refs
    mid = pieces[0].shape[0]
    for role in range(4):

        @pl.when(flags[ROLE] == role)
        def _(role=role):
            out[:mid] = pieces[2 * role][...]
            out[mid:] = pieces[2 * role + 1][...]

    @pl.when(flags[LAST] != 0)
    def _():
        rest = right.shape[1] - CROSS
        right[0] = wrap[: right.shape[1]]
        right[1, :rest] = wrap[right.shape[1] :]
        right[1, rest:] = cross[...]


def join(flags, wrap, cross, behind, *pieces):
    shape = pieces[0].shape
    return pl.pallas_call(
        join_kernel,
        out_shape=(
            jax.ShapeDtypeStruct((2 * shape[0],) + shape[1:], pieces[0].dtype),
            jax.ShapeDtypeStruct(behind.shape, behind.dtype),
        ),
        in_specs=[SMEM] + [VMEM] * (len(pieces) + 3),
        out_specs=(VMEM, VMEM),
        input_output_aliases={len(pieces) + 3: 1},
        compiler_params=pltpu.CompilerParams(vmem_limit_bytes=4 << 20),
        name="join",
    )(flags, *pieces, wrap, cross, behind)


def multiply_kernel(
    flags, om_ref, own, behind, mine, other, out_ref, table, tsm, todo, acc, wide, tsem
):
    rows, slots, size = out_ref.shape
    tiles = size // LANES
    sec = flags[SECTION]
    lane = lax.broadcasted_iota(jnp.int32, (rows, LANES), 1)
    low = lax.broadcasted_iota(jnp.int32, (2 * SUB, LANES), 1) < LANES // 2
    weight = jnp.zeros((rows, LANES), jnp.float32)
    for r in range(2 * HALF):
        weight = jnp.where((lane >> 2) == r, ((lane & 3) + 1).astype(jnp.float32) * 8.0**r, weight)
    weight = jnp.where(lane < 16, weight, 0.0)
    found = jnp.zeros((rows, LANES), jnp.float32)
    total = jnp.zeros((rows, 1), jnp.float32)
    om = om_ref[...]
    for s in range(2):
        right = own if s == 0 else behind
        rm = jnp.concatenate([right[0, rows, k] for k in range(HALF)], 0)
        lm = [
            jnp.concatenate([left[rows, k] for k in range(HALF)], 0)[:rows].astype(jnp.float32)
            for left in (mine, other)
        ]
        lm = jnp.where(sec == s, lm[0], lm[1])
        for k in range(HALF):
            e = jnp.sum(jnp.where(lane == LEFT + HALF * s + k, lm, 0.0), axis=1, keepdims=True)
            pick = (lane[:, : HALF * SUB].astype(jnp.float32) == e).astype(rm.dtype)
            got = jnp.dot(pick, rm, preferred_element_type=jnp.float32)
            code = jnp.sum(jnp.where(got == om, weight, 0.0), axis=1, keepdims=True)
            found = jnp.where(lane == s * HALF + k, code, found)
            found = jnp.where(lane == 8 + s * HALF + k, e, found)
            total = total + code
    found = jnp.where(lane == 4, total, found)
    table[...] = found.astype(jnp.int32)
    put = pltpu.make_async_copy(table, tsm, tsem)
    put.start()
    put.wait()

    def scan(i, n):
        def some(n):
            acc[i] = jnp.zeros(acc.shape[1:], acc.dtype)
            for c in range(2 * HALF):
                code = tsm[i, c]
                base = (i << 16) | (tsm[i, 8 + c] << 8) | (c << 5)
                for r in range(2 * HALF):
                    j = lax.shift_right_logical(code, 3 * r) & 7
                    todo[n] = base | (r << 3) | (j - 1)
                    n = n + (j != 0).astype(jnp.int32)
            return n

        return lax.cond(tsm[i, 4] != 0, some, lambda n: n, n)

    n_todo = lax.fori_loop(0, rows, scan, jnp.int32(0))
    for u in range(AHEAD):
        todo[n_todo + u] = rows << 16
    acc[rows] = jnp.zeros(acc.shape[1:], acc.dtype)

    def pairs(m, _):
        items = []
        for u in range(AHEAD):
            w = todo[m * AHEAD + u]
            i = lax.shift_right_logical(w, 16)
            e = lax.shift_right_logical(w, 8) & 63
            s = lax.shift_right_logical(w, 6) & 1
            k = lax.shift_right_logical(w, 5) & 1
            x = lax.shift_right_logical(w, 4) & 1
            h = lax.shift_right_logical(w, 3) & 1
            b = jnp.where(s == 0, own[x, e, h].astype(jnp.float32), behind[x, e, h].astype(jnp.float32))
            a = jnp.where(sec == s, mine[i, k].astype(jnp.float32), other[i, k].astype(jnp.float32))
            wide[u, pl.ds(0, SUB, stride=2), :] = b
            wide[u, pl.ds(1, SUB, stride=2), :] = pltpu.roll(b, LANES // 2, 1)
            items.append((i, w & 3, a.astype(mine.dtype)))
        sums = []
        for u, (_, _, a) in enumerate(items):
            v = wide[u]
            diag = jnp.concatenate(
                [jnp.where(low, v, 0.0), jnp.where(low, 0.0, pltpu.roll(v, LANES // 2, 1))], 0
            ).astype(mine.dtype)
            sums.append(jnp.dot(a, diag, preferred_element_type=jnp.float32))
        for (i, j, _), got in zip(items, sums):
            at = pl.ds(j, SUB, stride=slots)
            acc[i, at, :] = acc[i, at, :] + got
        return 0

    lax.fori_loop(0, (n_todo + AHEAD - 1) // AHEAD, pairs, 0)

    def finish(i, _):
        @pl.when(tsm[i, 4] == 0)
        def _():
            out_ref[i] = jnp.zeros(out_ref.shape[1:], out_ref.dtype)

        @pl.when(tsm[i, 4] != 0)
        def _():
            for t in range(tiles):
                out_ref[i, :, t * LANES : (t + 1) * LANES] = acc[
                    i, pl.ds(slots * t, slots), :
                ].astype(out_ref.dtype)

        return 0

    lax.fori_loop(0, rows, finish, 0)


def multiply(flags, om, own, behind, mine, other, slots):
    rows = om.shape[0]
    size = 2 * SUB * SUB * 2
    return pl.pallas_call(
        multiply_kernel,
        out_shape=jax.ShapeDtypeStruct((rows, slots, size), own.dtype),
        in_specs=[SMEM] + [VMEM] * 5,
        out_specs=VMEM,
        scratch_shapes=[
            pltpu.VMEM((rows, LANES), jnp.int32),
            pltpu.SMEM((rows, LANES), jnp.int32),
            pltpu.SMEM((rows * 4 * HALF * HALF + 2 * AHEAD,), jnp.int32),
            pltpu.VMEM((rows + 1, slots * size // LANES, LANES), jnp.float32),
            pltpu.VMEM((AHEAD, 2 * SUB, LANES), jnp.float32),
            pltpu.SemaphoreType.DMA,
        ],
        compiler_params=pltpu.CompilerParams(vmem_limit_bytes=12 << 20),
        name="multiply",
    )(flags, om, own, behind, mine, other)


def routes(n_row, n_col):
    to_a, to_b, to_core = [], [], []
    up, down, up_on, down_on = [], [], [], []
    for c in range(n_col):
        owner_a = c // 2
        owner_b = owner_a if c % 2 == 0 else (owner_a + 1) % n_row
        tree_b = owner_b ^ 1 if c % 2 == 0 else owner_b
        rank = lambda q: q * n_col + c
        to_a.append((rank(owner_a), rank(owner_a ^ 8)))
        to_b.append((rank(owner_b), rank(tree_b ^ 8)))
        if owner_b != tree_b:
            to_core.append((rank(owner_b), rank(tree_b)))
        for root in (owner_a, tree_b):
            for x in (0, 8):
                y = (root >> 1) & 3
                at = lambda d: rank((root & 8) ^ x | ((y + d) & 3) << 1 | root & 1)
                up.append((at(0), at(1)))
                down.append((at(0), at(3)))
                up_on.append((at(1), at(2)))
                down_on.append((at(3), at(2)))
    return to_a, to_b, to_core, up, down, up_on, down_on


def local(blocks, columns, counts, n_row, n_col):
    slots = columns.shape[1]
    p = lax.axis_index("col")
    q = lax.axis_index("row")
    k = p // 2
    even = p % 2 == 0
    root_a = k
    root_b = jnp.where(even, k ^ 1, (k + 1) % n_row)
    in_a = (q & 1) == (root_a & 1)
    root = jnp.where(in_a, root_a, root_b)
    role = (((q >> 1) & 3) - ((root >> 1) & 3)) & 3
    which = jnp.where(
        in_a,
        jnp.where(q == root_a, 0, 2),
        jnp.where(q == root_b, jnp.where(even, 4, 1), 3),
    )
    which = jnp.where(role == 0, which, -1)
    n_z = n_col // 2
    last = lambda i: (i + 1) % n_z == 0
    flags = [p % 2, which, role, p % n_z == 0, last(p), jnp.where(in_a, 0, 1)]
    flags = jnp.stack([v.astype(jnp.int32) for v in flags])

    table = jnp.concatenate([columns.T, counts.T], 0)
    tile, om = prep(flags, table, blocks)
    ga, gb = tile[0], tile[1]
    to_a, to_b, to_core, up_0, down_0, up_1, down_1 = routes(n_row, n_col)
    send = lambda v, route: lax.ppermute(v, ("row", "col"), route)

    from_next = [((i + 1) % n_col, i) for i in range(n_col)]
    behind = lax.ppermute(tile, "col", [pair for pair in from_next if not last(pair[1])])
    got_a = send(ga, to_a)
    got_b = send(gb, to_b)
    got_core = send(gb, to_core)
    got_a, got_b, got_core = lax.optimization_barrier((got_a, got_b, got_core))
    a, b, wrap, cross = pick(flags, tile, ga, gb, got_a, got_b, got_core)
    wrap = lax.ppermute(wrap, "col", [pair for pair in from_next if last(pair[1])])
    cross = lax.ppermute(cross, "col", [(0, n_z), (n_z, 0)])
    up = send(a, up_0)
    down = send(b, down_0)
    up, down, cross = lax.optimization_barrier((up, down, cross))
    c, d = turn(flags, a, b, up, down)
    up_2 = send(c, up_0 + up_1)
    down_2 = send(d, down_0 + down_1)
    cross = lax.ppermute(cross, "col", [(0, n_z - 1), (n_z, n_col - 1)])
    up_2, down_2, behind, wrap, cross = lax.optimization_barrier(
        (up_2, down_2, behind, wrap, cross)
    )
    mine, behind = join(flags, wrap, cross, behind, a, b, up, up_2, up_2, down_2, down_2, down)
    other = lax.ppermute(mine, "row", [(i, i ^ 1) for i in range(n_row)])
    return multiply(flags, om, tile, behind, mine, other, slots)


def solution(mesh):
    step = functools.partial(local, n_row=mesh.shape["row"], n_col=mesh.shape["col"])
    return jax.shard_map(
        step,
        mesh=mesh,
        in_specs=(P("col", "row", None), P("col", "row"), P("col", "row")),
        out_specs=P("col", "row", None),
        check_vma=False,
    )
```

time: 103 us -> 85.7 us (0.83)
  the two profiles are of different devices: /device:TPU:28 before, /device:TPU:1 now
where the time goes in v2:
time: 85.7 us; the launch traced here: 85.9 us
  starting transfers between devices  35.8 us (42%)
  waiting for transfers between devices  33 us (39%)
  Pallas kernels  14.4 us (17%)
  local copies, waits for them, and re-layouts  1.8 us (2%)
    ppermute x7, waiting for transfers between devices, local(): send = lambda v, route: lax.ppermute(v, ('row', 'col'), route)  24.6 us
    ppermute x1, starting transfers between devices, local(): cross = lax.ppermute(cross, 'col', [(0, n_z), (n_z, 0)])  17.1 us
    ppermute x7, starting transfers between devices, local(): send = lambda v, route: lax.ppermute(v, ('row', 'col'), route)  12.1 us
    pallas_call x1, Pallas kernels, multiply(): pl.pallas_call(multiply_kernel, out_shape=jax.ShapeDtypeStruct((rows, slo...  8.92 us
    ppermute x1, waiting for transfers between devices, local(): cross = lax.ppermute(cross, 'col', [(0, n_z - 1), (n_z, n_col - 1)])  6.5 us
    pallas_call x1, Pallas kernels, prep(): pl.pallas_call(prep_kernel, out_shape=(jax.ShapeDtypeStruct((2, rows + 2,...  3.52 us
    ppermute x1, starting transfers between devices, local(): other = lax.ppermute(mine, 'row', [(i, i ^ 1) for i in range(n_row)])  2.66 us
    ppermute x1, waiting for transfers between devices, local(): other = lax.ppermute(mine, 'row', [(i, i ^ 1) for i in range(n_row)])  1.94 us
  transfers between devices with their start and end apart: 12, of which 7 were waited for; matrix products, arithmetic and copies ran while one was open for 0% of the time, Pallas kernels for 2%

profile of v2, /device:TPU:1, one launch (start us, length us, event | category | flops | bytes accessed | tf_op | source)
XLA Modules:
  0.0 85.9 jit_solution(10581542550634159601)
XLA Ops:
  0.0 0.7 pad_add_fusion.table
  0.8 1.4 %copy-done = bf16[48,4,4096]{2,1,0:T(4,128)(2,1)S(1)} copy-done((bf16[48,4,4096]{2,1,0:T(4,128)(2,1)S(1)}, bf16[48,4,4096]{2,1,0:T(4,128)(2,1)}, u32[]{:S(2)}) %copy-start) | copy-done | bytes 1572888
  2.2 3.5 %prep.1 = (bf16[2,50,2,32,128]{4,3,2,1,0:T(8,128)(2,1)S(1)}, f32[48,128]{1,0:T(8,128)S(1)}) custom-call(s32[6]{0:T(128)S(1)} %stack.35.flags, s32[5,48]{1,0:T(8,128)S(1)} %pad_add_fusion.table, bf16[48,4,4096]{2,1,0:T(4,128)(2,1)S(1)} %copy-done), custom_call_target="tpu_custom_call" | custom-call | tf_op jit(solution)/shard_map/prep/pallas_call | solution.py:75
  6.0 0.7 collective-permute-start
  6.8 1.3 %collective-permute-start.2 = (bf16[50,2,32,128]{3,2,1,0:T(8,128)(2,1)S(1)}, bf16[50,2,32,128]{3,2,1,0:T(8,128)(2,1)S(1)}, u32[]{:S(2)}, u32[]{:S(2)}) collective-permute-start(bf16[50,2,32,128]{3,2,1,0:T(8,128)(2,1)S(1)} %get-tuple-element.47.refs_1_), channel_id=1, source_target_pairs={{0,32},{34,2},{68,100},{102,70},{136,168},{170,138},{204,236},{238... | collective-permute-start | bytes 2457608 | tf_op jit(solution)/shard_map/ppermute | solution.py:363
  8.1 0.7 collective-permute-start.1
  8.8 1.3 %collective-permute-start.8 = (bf16[2,50,2,32,128]{4,3,2,1,0:T(8,128)(2,1)S(1)}, bf16[2,50,2,32,128]{4,3,2,1,0:T(8,128)(2,1)S(1)}, u32[]{:S(2)}, u32[]{:S(2)}) collective-permute-start(bf16[2,50,2,32,128]{4,3,2,1,0:T(8,128)(2,1)S(1)} %get-tuple-element.27.refs_5_.own), channel_id=1, source_target_pairs={{1,0},{2,1},{3,2},{4,3},{5,4},{6,5},{7,6},{8,7},{9,8},{10,9},{11,1... | collective-permute-start | bytes 4915208 | tf_op jit(solution)/shard_map/ppermute | solution.py:366
  10.1 7.3 %collective-permute-done.2.refs_4_ = bf16[50,2,32,128]{3,2,1,0:T(8,128)(2,1)S(1)} collective-permute-done((bf16[50,2,32,128]{3,2,1,0:T(8,128)(2,1)S(1)}, bf16[50,2,32,128]{3,2,1,0:T(8,128)(2,1)S(1)}, u32[]{:S(2)}, u32[]{:S(2)}) %collective-permute-start.2) | collective-permute-done | bytes 819232 | tf_op jit(solution)/shard_map/ppermute | solution.py:363
  17.4 0.7 pick.1
  18.1 17.1 %collective-permute-start.5 = (bf16[35,2,32,128]{3,2,1,0:T(8,128)(2,1)S(1)}, bf16[35,2,32,128]{3,2,1,0:T(8,128)(2,1)S(1)}, u32[]{:S(2)}, u32[]{:S(2)}) collective-permute-start(bf16[35,2,32,128]{3,2,1,0:T(8,128)(2,1)S(1)} %get-tuple-element.33), channel_id=1, source_target_pairs={{0,16},{16,0},{32,48},{48,32},{64,80},{80,64},{96,112},{112,96},{1... | collective-permute-start | bytes 1720328 | tf_op jit(solution)/shard_map/ppermute | solution.py:373
  35.2 1.4 %collective-permute-start.9 = (bf16[65,2,32,128]{3,2,1,0:T(8,128)(2,1)S(1)}, bf16[65,2,32,128]{3,2,1,0:T(8,128)(2,1)S(1)}, u32[]{:S(2)}, u32[]{:S(2)}) collective-permute-start(bf16[65,2,32,128]{3,2,1,0:T(8,128)(2,1)S(1)} %get-tuple-element.38), channel_id=1, source_target_pairs={{16,15},{0,31},{48,47},{32,63},{80,79},{64,95},{112,111},{96,127},... | collective-permute-start | bytes 3194888 | tf_op jit(solution)/shard_map/ppermute | solution.py:372
  36.6 1.3 %collective-permute-start.3 = (bf16[25,2,32,128]{3,2,1,0:T(8,128)(2,1)S(1)}, bf16[25,2,32,128]{3,2,1,0:T(8,128)(2,1)S(1)}, u32[]{:S(2)}, u32[]{:S(2)}) collective-permute-start(bf16[25,2,32,128]{3,2,1,0:T(8,128)(2,1)S(1)} %get-tuple-element.31.a.refs_0_), channel_id=1, source_target_pairs={{0,64},{256,320},{32,96},{288,352},{1,65},{257,321},{33,97},{289,3... | collective-permute-start | bytes 1228808 | tf_op jit(solution)/shard_map/ppermute | solution.py:363
  37.9 2.4 %collective-permute-start.4 = (bf16[25,2,32,128]{3,2,1,0:T(8,128)(2,1)S(1)}, bf16[25,2,32,128]{3,2,1,0:T(8,128)(2,1)S(1)}, u32[]{:S(2)}, u32[]{:S(2)}) collective-permute-start(bf16[25,2,32,128]{3,2,1,0:T(8,128)(2,1)S(1)} %get-tuple-element.32.b.refs_1_), channel_id=1, source_target_pairs={{0,192},{256,448},{32,224},{288,480},{1,193},{257,449},{33,225},{2... | collective-permute-start | bytes 1228808 | tf_op jit(solution)/shard_map/ppermute | solution.py:363
  40.3 6.5 %collective-permute-done.3.up.refs_2_ = bf16[25,2,32,128]{3,2,1,0:T(8,128)(2,1)S(1)} collective-permute-done((bf16[25,2,32,128]{3,2,1,0:T(8,128)(2,1)S(1)}, bf16[25,2,32,128]{3,2,1,0:T(8,128)(2,1)S(1)}, u32[]{:S(2)}, u32[]{:S(2)}) %collective-permute-start.3) | collective-permute-done | bytes 409632 | tf_op jit(solution)/shard_map/ppermute | solution.py:363
  46.8 2.1 %collective-permute-done.4.down.refs_7_ = bf16[25,2,32,128]{3,2,1,0:T(8,128)(2,1)S(1)} collective-permute-done((bf16[25,2,32,128]{3,2,1,0:T(8,128)(2,1)S(1)}, bf16[25,2,32,128]{3,2,1,0:T(8,128)(2,1)S(1)}, u32[]{:S(2)}, u32[]{:S(2)}) %collective-permute-start.4) | collective-permute-done | bytes 409632 | tf_op jit(solution)/shard_map/ppermute | solution.py:363
  48.9 1.3 %collective-permute-start.10 = (bf16[35,2,32,128]{3,2,1,0:T(8,128)(2,1)S(1)}, bf16[35,2,32,128]{3,2,1,0:T(8,128)(2,1)S(1)}, u32[]{:S(2)}, u32[]{:S(2)}) collective-permute-start(bf16[35,2,32,128]{3,2,1,0:T(8,128)(2,1)S(1)} %collective-permute-done.5), channel_id=1, source_target_pairs={{0,15},{16,31},{32,47},{48,63},{64,79},{80,95},{96,111},{112,127},... | collective-permute-start | bytes 1720328 | tf_op jit(solution)/shard_map/ppermute | solution.py:380
  50.9 2.0 %collective-permute-start.6 = (bf16[25,2,32,128]{3,2,1,0:T(8,128)(2,1)S(1)}, bf16[25,2,32,128]{3,2,1,0:T(8,128)(2,1)S(1)}, u32[]{:S(2)}, u32[]{:S(2)}) collective-permute-start(bf16[25,2,32,128]{3,2,1,0:T(8,128)(2,1)S(1)} %get-tuple-element.36), channel_id=1, source_target_pairs={{0,64},{256,320},{32,96},{288,352},{1,65},{257,321},{33,97},{289,3... | collective-permute-start | bytes 1228808 | tf_op jit(solution)/shard_map/ppermute | solution.py:363
  52.9 3.7 %collective-permute-start.7 = (bf16[25,2,32,128]{3,2,1,0:T(8,128)(2,1)S(1)}, bf16[25,2,32,128]{3,2,1,0:T(8,128)(2,1)S(1)}, u32[]{:S(2)}, u32[]{:S(2)}) collective-permute-start(bf16[25,2,32,128]{3,2,1,0:T(8,128)(2,1)S(1)} %get-tuple-element.37), channel_id=1, source_target_pairs={{0,192},{256,448},{32,224},{288,480},{1,193},{257,449},{33,225},{2... | collective-permute-start | bytes 1228808 | tf_op jit(solution)/shard_map/ppermute | solution.py:363
  56.6 4.3 %collective-permute-done.6.refs_3_.refs_4_ = bf16[25,2,32,128]{3,2,1,0:T(8,128)(2,1)S(1)} collective-permute-done((bf16[25,2,32,128]{3,2,1,0:T(8,128)(2,1)S(1)}, bf16[25,2,32,128]{3,2,1,0:T(8,128)(2,1)S(1)}, u32[]{:S(2)}, u32[]{:S(2)}) %collective-permute-start.6) | collective-permute-done | bytes 409632 | tf_op jit(solution)/shard_map/ppermute | solution.py:363
  60.9 4.4 %collective-permute-done.7.refs_5_.refs_6_ = bf16[25,2,32,128]{3,2,1,0:T(8,128)(2,1)S(1)} collective-permute-done((bf16[25,2,32,128]{3,2,1,0:T(8,128)(2,1)S(1)}, bf16[25,2,32,128]{3,2,1,0:T(8,128)(2,1)S(1)}, u32[]{:S(2)}, u32[]{:S(2)}) %collective-permute-start.7) | collective-permute-done | bytes 409632 | tf_op jit(solution)/shard_map/ppermute | solution.py:363
  65.3 6.5 %collective-permute-done.10.refs_9_ = bf16[35,2,32,128]{3,2,1,0:T(8,128)(2,1)S(1)} collective-permute-done((bf16[35,2,32,128]{3,2,1,0:T(8,128)(2,1)S(1)}, bf16[35,2,32,128]{3,2,1,0:T(8,128)(2,1)S(1)}, u32[]{:S(2)}, u32[]{:S(2)}) %collective-permute-start.10) | collective-permute-done | bytes 573472 | tf_op jit(solution)/shard_map/ppermute | solution.py:380
  72.4 2.7 %collective-permute-start.11 = (bf16[50,2,32,128]{3,2,1,0:T(8,128)(2,1)S(1)}, bf16[50,2,32,128]{3,2,1,0:T(8,128)(2,1)S(1)}, u32[]{:S(2)}, u32[]{:S(2)}) collective-permute-start(bf16[50,2,32,128]{3,2,1,0:T(8,128)(2,1)S(1)} %get-tuple-element.46.mine), channel_id=1, source_target_pairs={{0,32},{32,0},{64,96},{96,64},{128,160},{160,128},{192,224},{224,1... | collective-permute-start | bytes 2457608 | tf_op jit(solution)/shard_map/ppermute | solution.py:385
  75.1 1.9 %collective-permute-done.11.other = bf16[50,2,32,128]{3,2,1,0:T(8,128)(2,1)S(1)} collective-permute-done((bf16[50,2,32,128]{3,2,1,0:T(8,128)(2,1)S(1)}, bf16[50,2,32,128]{3,2,1,0:T(8,128)(2,1)S(1)}, u32[]{:S(2)}, u32[]{:S(2)}) %collective-permute-start.11) | collective-permute-done | bytes 819232 | tf_op jit(solution)/shard_map/ppermute | solution.py:385
  77.0 8.9 %multiply.1 = bf16[48,4,4096]{2,1,0:T(4,128)(2,1)} custom-call(s32[6]{0:T(128)S(1)} %stack.35.flags, f32[48,128]{1,0:T(8,128)S(1)} %get-tuple-element.26.om_ref, bf16[2,50,2,32,128]{4,3,2,1,0:T(8,128)(2,1)S(1)} %get-tuple-element.27.refs_5_.own, bf16[2,50,2,32,128]{4,3,2,1,0:T(8,128)(2,1)S(1)} %get-tuple-element.45.behind, ...), custom_call_target="tpu_custom_call" | custom-call | tf_op jit(solution)/shard_map/multiply/pallas_call | solution.py:296
  (10 shorter events, 1.6 us)
Async XLA Ops:
  0.8 1.4 %copy-start = (bf16[48,4,4096]{2,1,0:T(4,128)(2,1)S(1)}, bf16[48,4,4096]{2,1,0:T(4,128)(2,1)}, u32[]{:S(2)}) copy-start(bf16[48,4,4096]{2,1,0:T(4,128)(2,1)} %tile.1) | copy-start | bytes 4718596
  6.0 4.0 %collective-permute-start = (bf16[50,2,32,128]{3,2,1,0:T(8,128)(2,1)S(1)}, bf16[50,2,32,128]{3,2,1,0:T(8,128)(2,1)S(1)}, u32[]{:S(2)}, u32[]{:S(2)}) collective-permute-start(bf16[50,2,32,128]{3,2,1,0:T(8,128)(2,1)S(1)} %get-tuple-element.48.refs_0_), channel_id=1, source_target_pairs={{0,256},{1,257},{34,290},{35,291},{68,324},{69,325},{102,358},{103... | collective-permute-start | bytes 2457608 | tf_op jit(solution)/shard_map/ppermute | solution.py:363
  6.8 10.6 %collective-permute-start.2 = (bf16[50,2,32,128]{3,2,1,0:T(8,128)(2,1)S(1)}, bf16[50,2,32,128]{3,2,1,0:T(8,128)(2,1)S(1)}, u32[]{:S(2)}, u32[]{:S(2)}) collective-permute-start(bf16[50,2,32,128]{3,2,1,0:T(8,128)(2,1)S(1)} %get-tuple-element.47.refs_1_), channel_id=1, source_target_pairs={{0,32},{34,2},{68,100},{102,70},{136,168},{170,138},{204,236},{238... | collective-permute-start | bytes 2457608 | tf_op jit(solution)/shard_map/ppermute | solution.py:363
  8.1 9.3 %collective-permute-start.1 = (bf16[50,2,32,128]{3,2,1,0:T(8,128)(2,1)S(1)}, bf16[50,2,32,128]{3,2,1,0:T(8,128)(2,1)S(1)}, u32[]{:S(2)}, u32[]{:S(2)}) collective-permute-start(bf16[50,2,32,128]{3,2,1,0:T(8,128)(2,1)S(1)} %get-tuple-element.47.refs_1_), channel_id=1, source_target_pairs={{0,288},{33,289},{34,258},{67,323},{68,356},{101,357},{102,326},{1... | collective-permute-start | bytes 2457608 | tf_op jit(solution)/shard_map/ppermute | solution.py:363
  8.8 47.8 %collective-permute-start.8 = (bf16[2,50,2,32,128]{4,3,2,1,0:T(8,128)(2,1)S(1)}, bf16[2,50,2,32,128]{4,3,2,1,0:T(8,128)(2,1)S(1)}, u32[]{:S(2)}, u32[]{:S(2)}) collective-permute-start(bf16[2,50,2,32,128]{4,3,2,1,0:T(8,128)(2,1)S(1)} %get-tuple-element.27.refs_5_.own), channel_id=1, source_target_pairs={{1,0},{2,1},{3,2},{4,3},{5,4},{6,5},{7,6},{8,7},{9,8},{10,9},{11,1... | collective-permute-start | bytes 4915208 | tf_op jit(solution)/shard_map/ppermute | solution.py:366
  18.1 30.8 %collective-permute-start.5 = (bf16[35,2,32,128]{3,2,1,0:T(8,128)(2,1)S(1)}, bf16[35,2,32,128]{3,2,1,0:T(8,128)(2,1)S(1)}, u32[]{:S(2)}, u32[]{:S(2)}) collective-permute-start(bf16[35,2,32,128]{3,2,1,0:T(8,128)(2,1)S(1)} %get-tuple-element.33), channel_id=1, source_target_pairs={{0,16},{16,0},{32,48},{48,32},{64,80},{80,64},{96,112},{112,96},{1... | collective-permute-start | bytes 1720328 | tf_op jit(solution)/shard_map/ppermute | solution.py:373
  35.2 30.0 %collective-permute-start.9 = (bf16[65,2,32,128]{3,2,1,0:T(8,128)(2,1)S(1)}, bf16[65,2,32,128]{3,2,1,0:T(8,128)(2,1)S(1)}, u32[]{:S(2)}, u32[]{:S(2)}) collective-permute-start(bf16[65,2,32,128]{3,2,1,0:T(8,128)(2,1)S(1)} %get-tuple-element.38), channel_id=1, source_target_pairs={{16,15},{0,31},{48,47},{32,63},{80,79},{64,95},{112,111},{96,127},... | collective-permute-start | bytes 3194888 | tf_op jit(solution)/shard_map/ppermute | solution.py:372
  36.6 10.2 %collective-permute-start.3 = (bf16[25,2,32,128]{3,2,1,0:T(8,128)(2,1)S(1)}, bf16[25,2,32,128]{3,2,1,0:T(8,128)(2,1)S(1)}, u32[]{:S(2)}, u32[]{:S(2)}) collective-permute-start(bf16[25,2,32,128]{3,2,1,0:T(8,128)(2,1)S(1)} %get-tuple-element.31.a.refs_0_), channel_id=1, source_target_pairs={{0,64},{256,320},{32,96},{288,352},{1,65},{257,321},{33,97},{289,3... | collective-permute-start | bytes 1228808 | tf_op jit(solution)/shard_map/ppermute | solution.py:363
  37.9 11.0 %collective-permute-start.4 = (bf16[25,2,32,128]{3,2,1,0:T(8,128)(2,1)S(1)}, bf16[25,2,32,128]{3,2,1,0:T(8,128)(2,1)S(1)}, u32[]{:S(2)}, u32[]{:S(2)}) collective-permute-start(bf16[25,2,32,128]{3,2,1,0:T(8,128)(2,1)S(1)} %get-tuple-element.32.b.refs_1_), channel_id=1, source_target_pairs={{0,192},{256,448},{32,224},{288,480},{1,193},{257,449},{33,225},{2... | collective-permute-start | bytes 1228808 | tf_op jit(solution)/shard_map/ppermute | solution.py:363
  48.9 22.8 %collective-permute-start.10 = (bf16[35,2,32,128]{3,2,1,0:T(8,128)(2,1)S(1)}, bf16[35,2,32,128]{3,2,1,0:T(8,128)(2,1)S(1)}, u32[]{:S(2)}, u32[]{:S(2)}) collective-permute-start(bf16[35,2,32,128]{3,2,1,0:T(8,128)(2,1)S(1)} %collective-permute-done.5), channel_id=1, source_target_pairs={{0,15},{16,31},{32,47},{48,63},{64,79},{80,95},{96,111},{112,127},... | collective-permute-start | bytes 1720328 | tf_op jit(solution)/shard_map/ppermute | solution.py:380
  50.9 10.0 %collective-permute-start.6 = (bf16[25,2,32,128]{3,2,1,0:T(8,128)(2,1)S(1)}, bf16[25,2,32,128]{3,2,1,0:T(8,128)(2,1)S(1)}, u32[]{:S(2)}, u32[]{:S(2)}) collective-permute-start(bf16[25,2,32,128]{3,2,1,0:T(8,128)(2,1)S(1)} %get-tuple-element.36), channel_id=1, source_target_pairs={{0,64},{256,320},{32,96},{288,352},{1,65},{257,321},{33,97},{289,3... | collective-permute-start | bytes 1228808 | tf_op jit(solution)/shard_map/ppermute | solution.py:363
  52.9 12.4 %collective-permute-start.7 = (bf16[25,2,32,128]{3,2,1,0:T(8,128)(2,1)S(1)}, bf16[25,2,32,128]{3,2,1,0:T(8,128)(2,1)S(1)}, u32[]{:S(2)}, u32[]{:S(2)}) collective-permute-start(bf16[25,2,32,128]{3,2,1,0:T(8,128)(2,1)S(1)} %get-tuple-element.37), channel_id=1, source_target_pairs={{0,192},{256,448},{32,224},{288,480},{1,193},{257,449},{33,225},{2... | collective-permute-start | bytes 1228808 | tf_op jit(solution)/shard_map/ppermute | solution.py:363
  72.4 4.6 %collective-permute-start.11 = (bf16[50,2,32,128]{3,2,1,0:T(8,128)(2,1)S(1)}, bf16[50,2,32,128]{3,2,1,0:T(8,128)(2,1)S(1)}, u32[]{:S(2)}, u32[]{:S(2)}) collective-permute-start(bf16[50,2,32,128]{3,2,1,0:T(8,128)(2,1)S(1)} %get-tuple-element.46.mine), channel_id=1, source_target_pairs={{0,32},{32,0},{64,96},{96,64},{128,160},{160,128},{192,224},{224,1... | collective-permute-start | bytes 2457608 | tf_op jit(solution)/shard_map/ppermute | solution.py:385

commit v3 on v2

--- a/solution.py
+++ b/solution.py
@@ -10,7 +10,7 @@
 HALF = 2
 SUB = 32
 LANES = 128
-AHEAD = 4
+AHEAD = 6
 FIRST, WHICH, ROLE, HEAD, LAST, SECTION = range(6)
 CROSS = 35
 LEFT = 32
@@ -188,12 +188,14 @@
     )(flags, *pieces, wrap, cross, behind)
 
 
-def multiply_kernel(
-    flags, om_ref, own, behind, mine, other, out_ref, table, tsm, todo, acc, wide, tsem
-):
-    rows, slots, size = out_ref.shape
-    tiles = size // LANES
-    sec = flags[SECTION]
+def multiply_kernel(phase, flags, om_ref, own, behind, left, *refs):
+    if phase == 0:
+        acc, found_ref, tsm, todo, table, wide, tsem = refs
+    else:
+        before, _, out_ref, acc, tsm, todo, table, wide, tsem = refs
+    rows = om_ref.shape[0]
+    slots = 2 * HALF
+    s = flags[SECTION] if phase == 0 else 1 - flags[SECTION]
     lane = lax.broadcasted_iota(jnp.int32, (rows, LANES), 1)
     low = lax.broadcasted_iota(jnp.int32, (2 * SUB, LANES), 1) < LANES // 2
     weight = jnp.zeros((rows, LANES), jnp.float32)
@@ -203,23 +205,24 @@
     found = jnp.zeros((rows, LANES), jnp.float32)
     total = jnp.zeros((rows, 1), jnp.float32)
     om = om_ref[...]
-    for s in range(2):
-        right = own if s == 0 else behind
-        rm = jnp.concatenate([right[0, rows, k] for k in range(HALF)], 0)
-        lm = [
-            jnp.concatenate([left[rows, k] for k in range(HALF)], 0)[:rows].astype(jnp.float32)
-            for left in (mine, other)
-        ]
-        lm = jnp.where(sec == s, lm[0], lm[1])
-        for k in range(HALF):
-            e = jnp.sum(jnp.where(lane == LEFT + HALF * s + k, lm, 0.0), axis=1, keepdims=True)
-            pick = (lane[:, : HALF * SUB].astype(jnp.float32) == e).astype(rm.dtype)
-            got = jnp.dot(pick, rm, preferred_element_type=jnp.float32)
-            code = jnp.sum(jnp.where(got == om, weight, 0.0), axis=1, keepdims=True)
-            found = jnp.where(lane == s * HALF + k, code, found)
-            found = jnp.where(lane == 8 + s * HALF + k, e, found)
-            total = total + code
+    index = lambda ref: jnp.concatenate([ref(k) for k in range(HALF)], 0).astype(jnp.float32)
+    rm = jnp.where(s == 0, index(lambda k: own[0, rows, k]), index(lambda k: behind[0, rows, k]))
+    rm = rm.astype(own.dtype)
+    lm = index(lambda k: left[rows, k])[:rows]
+    for k in range(HALF):
+        e = jnp.sum(jnp.where(lane == LEFT + HALF * s + k, lm, 0.0), axis=1, keepdims=True)
+        pick = (lane[:, : HALF * SUB].astype(jnp.float32) == e).astype(rm.dtype)
+        got = jnp.dot(pick, rm, preferred_element_type=jnp.float32)
+        code = jnp.sum(jnp.where(got == om, weight, 0.0), axis=1, keepdims=True)
+        found = jnp.where(lane == k, code, found)
+        found = jnp.where(lane == 8 + k, e, found)
+        total = total + code
     found = jnp.where(lane == 4, total, found)
+    if phase == 0:
+        found_ref[...] = found
+    else:
+        was = jnp.sum(jnp.where(lane == 4, before[...], 0.0), axis=1, keepdims=True)
+        found = jnp.where(lane == 5, was, jnp.where(lane == 6, was + total, found))
     table[...] = found.astype(jnp.int32)
     put = pltpu.make_async_copy(table, tsm, tsem)
     put.start()
@@ -227,10 +230,16 @@
 
     def scan(i, n):
         def some(n):
-            acc[i] = jnp.zeros(acc.shape[1:], acc.dtype)
-            for c in range(2 * HALF):
-                code = tsm[i, c]
-                base = (i << 16) | (tsm[i, 8 + c] << 8) | (c << 5)
+            def clear():
+                acc[i] = jnp.zeros(acc.shape[1:], acc.dtype)
+
+            if phase == 0:
+                clear()
+            else:
+                pl.when(tsm[i, 5] == 0)(clear)
+            for k in range(HALF):
+                code = tsm[i, k]
+                base = (i << 16) | (tsm[i, 8 + k] << 8) | (k << 5)
                 for r in range(2 * HALF):
                     j = lax.shift_right_logical(code, 3 * r) & 7
                     todo[n] = base | (r << 3) | (j - 1)
@@ -239,7 +248,7 @@
 
         return lax.cond(tsm[i, 4] != 0, some, lambda n: n, n)
 
-    n_todo = lax.fori_loop(0, rows, scan, jnp.int32(0))
+    n_todo = lax.fori_loop(0, rows, scan, jnp.int32(0), unroll=4)
     for u in range(AHEAD):
         todo[n_todo + u] = rows << 16
     acc[rows] = jnp.zeros(acc.shape[1:], acc.dtype)
@@ -250,21 +259,19 @@
             w = todo[m * AHEAD + u]
             i = lax.shift_right_logical(w, 16)
             e = lax.shift_right_logical(w, 8) & 63
-            s = lax.shift_right_logical(w, 6) & 1
             k = lax.shift_right_logical(w, 5) & 1
             x = lax.shift_right_logical(w, 4) & 1
             h = lax.shift_right_logical(w, 3) & 1
             b = jnp.where(s == 0, own[x, e, h].astype(jnp.float32), behind[x, e, h].astype(jnp.float32))
-            a = jnp.where(sec == s, mine[i, k].astype(jnp.float32), other[i, k].astype(jnp.float32))
             wide[u, pl.ds(0, SUB, stride=2), :] = b
             wide[u, pl.ds(1, SUB, stride=2), :] = pltpu.roll(b, LANES // 2, 1)
-            items.append((i, w & 3, a.astype(mine.dtype)))
+            items.append((i, w & 3, left[i, k]))
         sums = []
         for u, (_, _, a) in enumerate(items):
             v = wide[u]
             diag = jnp.concatenate(
                 [jnp.where(low, v, 0.0), jnp.where(low, 0.0, pltpu.roll(v, LANES // 2, 1))], 0
-            ).astype(mine.dtype)
+            ).astype(left.dtype)
             sums.append(jnp.dot(a, diag, preferred_element_type=jnp.float32))
         for (i, j, _), got in zip(items, sums):
             at = pl.ds(j, SUB, stride=slots)
@@ -273,42 +280,51 @@
 
     lax.fori_loop(0, (n_todo + AHEAD - 1) // AHEAD, pairs, 0)
 
+    if phase == 0:
+        return
+
     def finish(i, _):
-        @pl.when(tsm[i, 4] == 0)
+        @pl.when(tsm[i, 6] == 0)
         def _():
             out_ref[i] = jnp.zeros(out_ref.shape[1:], out_ref.dtype)
 
-        @pl.when(tsm[i, 4] != 0)
+        @pl.when(tsm[i, 6] != 0)
         def _():
-            for t in range(tiles):
+            for t in range(out_ref.shape[2] // LANES):
                 out_ref[i, :, t * LANES : (t + 1) * LANES] = acc[
                     i, pl.ds(slots * t, slots), :
                 ].astype(out_ref.dtype)
 
         return 0
 
-    lax.fori_loop(0, rows, finish, 0)
-
-
-def multiply(flags, om, own, behind, mine, other, slots):
+    lax.fori_loop(0, rows, finish, 0, unroll=4)
+
+
+def multiply(phase, flags, om, own, behind, left, *sums):
     rows = om.shape[0]
-    size = 2 * SUB * SUB * 2
+    slots = 2 * HALF
+    size = SUB * LANES
+    acc = jax.ShapeDtypeStruct((rows + 1, slots * size // LANES, LANES), jnp.float32)
+    out = (acc, jax.ShapeDtypeStruct(om.shape, om.dtype))
+    if phase:
+        out = (jax.ShapeDtypeStruct((rows, slots, size), own.dtype), acc)
     return pl.pallas_call(
-        multiply_kernel,
-        out_shape=jax.ShapeDtypeStruct((rows, slots, size), own.dtype),
-        in_specs=[SMEM] + [VMEM] * 5,
-        out_specs=VMEM,
+        functools.partial(multiply_kernel, phase),
+        out_shape=out,
+        in_specs=[SMEM] + [VMEM] * (4 + len(sums)),
+        out_specs=(VMEM, VMEM),
         scratch_shapes=[
+            pltpu.SMEM((rows, LANES), jnp.int32),
+            pltpu.SMEM((rows * slots * HALF + 2 * AHEAD,), jnp.int32),
             pltpu.VMEM((rows, LANES), jnp.int32),
-            pltpu.SMEM((rows, LANES), jnp.int32),
-            pltpu.SMEM((rows * 4 * HALF * HALF + 2 * AHEAD,), jnp.int32),
-            pltpu.VMEM((rows + 1, slots * size // LANES, LANES), jnp.float32),
             pltpu.VMEM((AHEAD, 2 * SUB, LANES), jnp.float32),
             pltpu.SemaphoreType.DMA,
         ],
+        input_output_aliases={6: 1} if phase else {},
         compiler_params=pltpu.CompilerParams(vmem_limit_bytes=12 << 20),
-        name="multiply",
-    )(flags, om, own, behind, mine, other)
+        cost_estimate=pl.CostEstimate(flops=10**9, bytes_accessed=4 << 20, transcendentals=0),
+        name="multiply%d" % phase,
+    )(flags, om, own, behind, left, *sums)
 
 
 def routes(n_row, n_col):
@@ -335,7 +351,6 @@
 
 
 def local(blocks, columns, counts, n_row, n_col):
-    slots = columns.shape[1]
     p = lax.axis_index("col")
     q = lax.axis_index("row")
     k = p // 2
@@ -383,7 +398,8 @@
     )
     mine, behind = join(flags, wrap, cross, behind, a, b, up, up_2, up_2, down_2, down_2, down)
     other = lax.ppermute(mine, "row", [(i, i ^ 1) for i in range(n_row)])
-    return multiply(flags, om, tile, behind, mine, other, slots)
+    sums, found = multiply(0, flags, om, tile, behind, mine)
+    return multiply(1, flags, om, tile, behind, other, found, sums)[0]
 
 
 def solution(mesh):

time: 85.7 us -> 84.9 us (level)
  waiting for transfers between devices: 33 us -> 31.1 us
    ppermute x1, waiting for transfers between devices: 1.94 us -> 0.01 us  [local(): other = lax.ppermute(mine, 'row', [(i, i ^ 1) for i in range(n_row)])]
    pallas_call x1 -> x2, Pallas kernels: 8.92 us -> 9.43 us  [multiply(): pl.pallas_call(functools.partial(multiply_kernel, phase), out_shape=out,...]
  transfers between devices with their start and end apart: 12 -> 12, of which waited for: 7 -> 6; matrix products, arithmetic and copies ran while one was open for 0% -> 0% of each run, Pallas kernels for 2% -> 5%
where the time goes in v3:
time: 84.9 us; the launch traced here: 84.5 us
  starting transfers between devices  35.8 us (42%)
  waiting for transfers between devices  31.1 us (37%)
  Pallas kernels  14.9 us (18%)
  local copies, waits for them, and re-layouts  1.8 us (2%)
    ppermute x7, waiting for transfers between devices, local(): send = lambda v, route: lax.ppermute(v, ('row', 'col'), route)  24.6 us
    ppermute x1, starting transfers between devices, local(): cross = lax.ppermute(cross, 'col', [(0, n_z), (n_z, 0)])  17.1 us
    ppermute x7, starting transfers between devices, local(): send = lambda v, route: lax.ppermute(v, ('row', 'col'), route)  12.1 us
    pallas_call x2, Pallas kernels, multiply(): pl.pallas_call(functools.partial(multiply_kernel, phase), out_shape=out,...  9.43 us
    ppermute x1, waiting for transfers between devices, local(): cross = lax.ppermute(cross, 'col', [(0, n_z - 1), (n_z, n_col - 1)])  6.5 us
    pallas_call x1, Pallas kernels, prep(): pl.pallas_call(prep_kernel, out_shape=(jax.ShapeDtypeStruct((2, rows + 2,...  3.52 us
    ppermute x1, starting transfers between devices, local(): other = lax.ppermute(mine, 'row', [(i, i ^ 1) for i in range(n_row)])  2.66 us
  transfers between devices with their start and end apart: 12, of which 6 were waited for; matrix products, arithmetic and copies ran while one was open for 0% of the time, Pallas kernels for 5%

profile of v3, /device:TPU:1, one launch (start us, length us, event | category | flops | bytes accessed | tf_op | source)
XLA Modules:
  0.0 84.5 jit_solution(9544644166290260503)
XLA Ops:
  0.0 0.7 pad_add_fusion.table
  0.8 1.4 %copy-done = bf16[48,4,4096]{2,1,0:T(4,128)(2,1)S(1)} copy-done((bf16[48,4,4096]{2,1,0:T(4,128)(2,1)S(1)}, bf16[48,4,4096]{2,1,0:T(4,128)(2,1)}, u32[]{:S(2)}) %copy-start) | copy-done | bytes 1572888
  2.2 3.5 %prep.1 = (bf16[2,50,2,32,128]{4,3,2,1,0:T(8,128)(2,1)S(1)}, f32[48,128]{1,0:T(8,128)S(1)}) custom-call(s32[6]{0:T(128)S(1)} %stack.35.flags, s32[5,48]{1,0:T(8,128)S(1)} %pad_add_fusion.table, bf16[48,4,4096]{2,1,0:T(4,128)(2,1)S(1)} %copy-done), custom_call_target="tpu_custom_call" | custom-call | tf_op jit(solution)/shard_map/prep/pallas_call | solution.py:75
  6.0 0.7 collective-permute-start
  6.8 1.3 %collective-permute-start.2 = (bf16[50,2,32,128]{3,2,1,0:T(8,128)(2,1)S(1)}, bf16[50,2,32,128]{3,2,1,0:T(8,128)(2,1)S(1)}, u32[]{:S(2)}, u32[]{:S(2)}) collective-permute-start(bf16[50,2,32,128]{3,2,1,0:T(8,128)(2,1)S(1)} %get-tuple-element.53.refs_1_), channel_id=1, source_target_pairs={{0,32},{34,2},{68,100},{102,70},{136,168},{170,138},{204,236},{238... | collective-permute-start | bytes 2457608 | tf_op jit(solution)/shard_map/ppermute | solution.py:378
  8.1 0.7 collective-permute-start.1
  8.8 1.3 %collective-permute-start.8 = (bf16[2,50,2,32,128]{4,3,2,1,0:T(8,128)(2,1)S(1)}, bf16[2,50,2,32,128]{4,3,2,1,0:T(8,128)(2,1)S(1)}, u32[]{:S(2)}, u32[]{:S(2)}) collective-permute-start(bf16[2,50,2,32,128]{4,3,2,1,0:T(8,128)(2,1)S(1)} %get-tuple-element.30.refs_5_.own), channel_id=1, source_target_pairs={{1,0},{2,1},{3,2},{4,3},{5,4},{6,5},{7,6},{8,7},{9,8},{10,9},{11,1... | collective-permute-start | bytes 4915208 | tf_op jit(solution)/shard_map/ppermute | solution.py:381
  10.1 7.3 %collective-permute-done.2.refs_4_ = bf16[50,2,32,128]{3,2,1,0:T(8,128)(2,1)S(1)} collective-permute-done((bf16[50,2,32,128]{3,2,1,0:T(8,128)(2,1)S(1)}, bf16[50,2,32,128]{3,2,1,0:T(8,128)(2,1)S(1)}, u32[]{:S(2)}, u32[]{:S(2)}) %collective-permute-start.2) | collective-permute-done | bytes 819232 | tf_op jit(solution)/shard_map/ppermute | solution.py:378
  17.4 0.7 pick.1
  18.1 17.1 %collective-permute-start.5 = (bf16[35,2,32,128]{3,2,1,0:T(8,128)(2,1)S(1)}, bf16[35,2,32,128]{3,2,1,0:T(8,128)(2,1)S(1)}, u32[]{:S(2)}, u32[]{:S(2)}) collective-permute-start(bf16[35,2,32,128]{3,2,1,0:T(8,128)(2,1)S(1)} %get-tuple-element.36), channel_id=1, source_target_pairs={{0,16},{16,0},{32,48},{48,32},{64,80},{80,64},{96,112},{112,96},{1... | collective-permute-start | bytes 1720328 | tf_op jit(solution)/shard_map/ppermute | solution.py:388
  35.2 1.4 %collective-permute-start.9 = (bf16[65,2,32,128]{3,2,1,0:T(8,128)(2,1)S(1)}, bf16[65,2,32,128]{3,2,1,0:T(8,128)(2,1)S(1)}, u32[]{:S(2)}, u32[]{:S(2)}) collective-permute-start(bf16[65,2,32,128]{3,2,1,0:T(8,128)(2,1)S(1)} %get-tuple-element.41), channel_id=1, source_target_pairs={{16,15},{0,31},{48,47},{32,63},{80,79},{64,95},{112,111},{96,127},... | collective-permute-start | bytes 3194888 | tf_op jit(solution)/shard_map/ppermute | solution.py:387
  36.6 1.3 %collective-permute-start.3 = (bf16[25,2,32,128]{3,2,1,0:T(8,128)(2,1)S(1)}, bf16[25,2,32,128]{3,2,1,0:T(8,128)(2,1)S(1)}, u32[]{:S(2)}, u32[]{:S(2)}) collective-permute-start(bf16[25,2,32,128]{3,2,1,0:T(8,128)(2,1)S(1)} %get-tuple-element.34.a.refs_0_), channel_id=1, source_target_pairs={{0,64},{256,320},{32,96},{288,352},{1,65},{257,321},{33,97},{289,3... | collective-permute-start | bytes 1228808 | tf_op jit(solution)/shard_map/ppermute | solution.py:378
  37.9 2.4 %collective-permute-start.4 = (bf16[25,2,32,128]{3,2,1,0:T(8,128)(2,1)S(1)}, bf16[25,2,32,128]{3,2,1,0:T(8,128)(2,1)S(1)}, u32[]{:S(2)}, u32[]{:S(2)}) collective-permute-start(bf16[25,2,32,128]{3,2,1,0:T(8,128)(2,1)S(1)} %get-tuple-element.35.b.refs_1_), channel_id=1, source_target_pairs={{0,192},{256,448},{32,224},{288,480},{1,193},{257,449},{33,225},{2... | collective-permute-start | bytes 1228808 | tf_op jit(solution)/shard_map/ppermute | solution.py:378
  40.3 6.5 %collective-permute-done.3.up.refs_2_ = bf16[25,2,32,128]{3,2,1,0:T(8,128)(2,1)S(1)} collective-permute-done((bf16[25,2,32,128]{3,2,1,0:T(8,128)(2,1)S(1)}, bf16[25,2,32,128]{3,2,1,0:T(8,128)(2,1)S(1)}, u32[]{:S(2)}, u32[]{:S(2)}) %collective-permute-start.3) | collective-permute-done | bytes 409632 | tf_op jit(solution)/shard_map/ppermute | solution.py:378
  46.8 2.1 %collective-permute-done.4.down.refs_7_ = bf16[25,2,32,128]{3,2,1,0:T(8,128)(2,1)S(1)} collective-permute-done((bf16[25,2,32,128]{3,2,1,0:T(8,128)(2,1)S(1)}, bf16[25,2,32,128]{3,2,1,0:T(8,128)(2,1)S(1)}, u32[]{:S(2)}, u32[]{:S(2)}) %collective-permute-start.4) | collective-permute-done | bytes 409632 | tf_op jit(solution)/shard_map/ppermute | solution.py:378
  48.9 1.3 %collective-permute-start.10 = (bf16[35,2,32,128]{3,2,1,0:T(8,128)(2,1)S(1)}, bf16[35,2,32,128]{3,2,1,0:T(8,128)(2,1)S(1)}, u32[]{:S(2)}, u32[]{:S(2)}) collective-permute-start(bf16[35,2,32,128]{3,2,1,0:T(8,128)(2,1)S(1)} %collective-permute-done.5), channel_id=1, source_target_pairs={{0,15},{16,31},{32,47},{48,63},{64,79},{80,95},{96,111},{112,127},... | collective-permute-start | bytes 1720328 | tf_op jit(solution)/shard_map/ppermute | solution.py:395
  50.9 2.0 %collective-permute-start.6 = (bf16[25,2,32,128]{3,2,1,0:T(8,128)(2,1)S(1)}, bf16[25,2,32,128]{3,2,1,0:T(8,128)(2,1)S(1)}, u32[]{:S(2)}, u32[]{:S(2)}) collective-permute-start(bf16[25,2,32,128]{3,2,1,0:T(8,128)(2,1)S(1)} %get-tuple-element.39), channel_id=1, source_target_pairs={{0,64},{256,320},{32,96},{288,352},{1,65},{257,321},{33,97},{289,3... | collective-permute-start | bytes 1228808 | tf_op jit(solution)/shard_map/ppermute | solution.py:378
  52.9 3.7 %collective-permute-start.7 = (bf16[25,2,32,128]{3,2,1,0:T(8,128)(2,1)S(1)}, bf16[25,2,32,128]{3,2,1,0:T(8,128)(2,1)S(1)}, u32[]{:S(2)}, u32[]{:S(2)}) collective-permute-start(bf16[25,2,32,128]{3,2,1,0:T(8,128)(2,1)S(1)} %get-tuple-element.40), channel_id=1, source_target_pairs={{0,192},{256,448},{32,224},{288,480},{1,193},{257,449},{33,225},{2... | collective-permute-start | bytes 1228808 | tf_op jit(solution)/shard_map/ppermute | solution.py:378
  56.6 4.3 %collective-permute-done.6.refs_3_.refs_4_ = bf16[25,2,32,128]{3,2,1,0:T(8,128)(2,1)S(1)} collective-permute-done((bf16[25,2,32,128]{3,2,1,0:T(8,128)(2,1)S(1)}, bf16[25,2,32,128]{3,2,1,0:T(8,128)(2,1)S(1)}, u32[]{:S(2)}, u32[]{:S(2)}) %collective-permute-start.6) | collective-permute-done | bytes 409632 | tf_op jit(solution)/shard_map/ppermute | solution.py:378
  60.9 4.4 %collective-permute-done.7.refs_5_.refs_6_ = bf16[25,2,32,128]{3,2,1,0:T(8,128)(2,1)S(1)} collective-permute-done((bf16[25,2,32,128]{3,2,1,0:T(8,128)(2,1)S(1)}, bf16[25,2,32,128]{3,2,1,0:T(8,128)(2,1)S(1)}, u32[]{:S(2)}, u32[]{:S(2)}) %collective-permute-start.7) | collective-permute-done | bytes 409632 | tf_op jit(solution)/shard_map/ppermute | solution.py:378
  65.3 6.5 %collective-permute-done.10.refs_9_ = bf16[35,2,32,128]{3,2,1,0:T(8,128)(2,1)S(1)} collective-permute-done((bf16[35,2,32,128]{3,2,1,0:T(8,128)(2,1)S(1)}, bf16[35,2,32,128]{3,2,1,0:T(8,128)(2,1)S(1)}, u32[]{:S(2)}, u32[]{:S(2)}) %collective-permute-start.10) | collective-permute-done | bytes 573472 | tf_op jit(solution)/shard_map/ppermute | solution.py:395
  72.4 2.7 %collective-permute-start.11 = (bf16[50,2,32,128]{3,2,1,0:T(8,128)(2,1)S(1)}, bf16[50,2,32,128]{3,2,1,0:T(8,128)(2,1)S(1)}, u32[]{:S(2)}, u32[]{:S(2)}) collective-permute-start(bf16[50,2,32,128]{3,2,1,0:T(8,128)(2,1)S(1)} %get-tuple-element.49.left), channel_id=1, source_target_pairs={{0,32},{32,0},{64,96},{96,64},{128,160},{160,128},{192,224},{224,1... | collective-permute-start | bytes 2457608 | tf_op jit(solution)/shard_map/ppermute | solution.py:400
  75.1 3.2 %multiply0.1 = (f32[49,128,128]{2,1,0:T(8,128)S(1)}, f32[48,128]{1,0:T(8,128)S(1)}) custom-call(s32[6]{0:T(128)S(1)} %stack.35.flags, f32[48,128]{1,0:T(8,128)S(1)} %get-tuple-element.29.om_ref, bf16[2,50,2,32,128]{4,3,2,1,0:T(8,128)(2,1)S(1)} %get-tuple-element.30.refs_5_.own, bf16[2,50,2,32,128]{4,3,2,1,0:T(8,128)(2,1)S(1)} %get-tuple-element.48.behind, ...), custom_call_target="tpu_custom_call" | custom-call | flops 1000000000 | bytes 4194304 | tf_op jit(solution)/shard_map/multiply0/pallas_call | solution.py:311
  78.3 6.2 %multiply1.1 = (bf16[48,4,4096]{2,1,0:T(4,128)(2,1)}, f32[49,128,128]{2,1,0:T(8,128)S(1)}) custom-call(s32[6]{0:T(128)S(1)} %stack.35.flags, f32[48,128]{1,0:T(8,128)S(1)} %get-tuple-element.29.om_ref, bf16[2,50,2,32,128]{4,3,2,1,0:T(8,128)(2,1)S(1)} %get-tuple-element.30.refs_5_.own, ...), custom_call_target="tpu_custom_call", output_to_operand_aliasing={{1}: (6, {})} | custom-call | flops 1000000000 | bytes 4194304 | tf_op jit(solution)/shard_map/multiply1/pallas_call | solution.py:311
  (11 shorter events, 1.6 us)
Async XLA Ops:
  0.8 1.4 %copy-start = (bf16[48,4,4096]{2,1,0:T(4,128)(2,1)S(1)}, bf16[48,4,4096]{2,1,0:T(4,128)(2,1)}, u32[]{:S(2)}) copy-start(bf16[48,4,4096]{2,1,0:T(4,128)(2,1)} %tile.1) | copy-start | bytes 4718596
  6.0 4.0 %collective-permute-start = (bf16[50,2,32,128]{3,2,1,0:T(8,128)(2,1)S(1)}, bf16[50,2,32,128]{3,2,1,0:T(8,128)(2,1)S(1)}, u32[]{:S(2)}, u32[]{:S(2)}) collective-permute-start(bf16[50,2,32,128]{3,2,1,0:T(8,128)(2,1)S(1)} %get-tuple-element.54.refs_0_), channel_id=1, source_target_pairs={{0,256},{1,257},{34,290},{35,291},{68,324},{69,325},{102,358},{103... | collective-permute-start | bytes 2457608 | tf_op jit(solution)/shard_map/ppermute | solution.py:378
  6.8 10.6 %collective-permute-start.2 = (bf16[50,2,32,128]{3,2,1,0:T(8,128)(2,1)S(1)}, bf16[50,2,32,128]{3,2,1,0:T(8,128)(2,1)S(1)}, u32[]{:S(2)}, u32[]{:S(2)}) collective-permute-start(bf16[50,2,32,128]{3,2,1,0:T(8,128)(2,1)S(1)} %get-tuple-element.53.refs_1_), channel_id=1, source_target_pairs={{0,32},{34,2},{68,100},{102,70},{136,168},{170,138},{204,236},{238... | collective-permute-start | bytes 2457608 | tf_op jit(solution)/shard_map/ppermute | solution.py:378
  8.1 9.3 %collective-permute-start.1 = (bf16[50,2,32,128]{3,2,1,0:T(8,128)(2,1)S(1)}, bf16[50,2,32,128]{3,2,1,0:T(8,128)(2,1)S(1)}, u32[]{:S(2)}, u32[]{:S(2)}) collective-permute-start(bf16[50,2,32,128]{3,2,1,0:T(8,128)(2,1)S(1)} %get-tuple-element.53.refs_1_), channel_id=1, source_target_pairs={{0,288},{33,289},{34,258},{67,323},{68,356},{101,357},{102,326},{1... | collective-permute-start | bytes 2457608 | tf_op jit(solution)/shard_map/ppermute | solution.py:378
  8.8 47.8 %collective-permute-start.8 = (bf16[2,50,2,32,128]{4,3,2,1,0:T(8,128)(2,1)S(1)}, bf16[2,50,2,32,128]{4,3,2,1,0:T(8,128)(2,1)S(1)}, u32[]{:S(2)}, u32[]{:S(2)}) collective-permute-start(bf16[2,50,2,32,128]{4,3,2,1,0:T(8,128)(2,1)S(1)} %get-tuple-element.30.refs_5_.own), channel_id=1, source_target_pairs={{1,0},{2,1},{3,2},{4,3},{5,4},{6,5},{7,6},{8,7},{9,8},{10,9},{11,1... | collective-permute-start | bytes 4915208 | tf_op jit(solution)/shard_map/ppermute | solution.py:381
  18.1 30.8 %collective-permute-start.5 = (bf16[35,2,32,128]{3,2,1,0:T(8,128)(2,1)S(1)}, bf16[35,2,32,128]{3,2,1,0:T(8,128)(2,1)S(1)}, u32[]{:S(2)}, u32[]{:S(2)}) collective-permute-start(bf16[35,2,32,128]{3,2,1,0:T(8,128)(2,1)S(1)} %get-tuple-element.36), channel_id=1, source_target_pairs={{0,16},{16,0},{32,48},{48,32},{64,80},{80,64},{96,112},{112,96},{1... | collective-permute-start | bytes 1720328 | tf_op jit(solution)/shard_map/ppermute | solution.py:388
  35.2 30.0 %collective-permute-start.9 = (bf16[65,2,32,128]{3,2,1,0:T(8,128)(2,1)S(1)}, bf16[65,2,32,128]{3,2,1,0:T(8,128)(2,1)S(1)}, u32[]{:S(2)}, u32[]{:S(2)}) collective-permute-start(bf16[65,2,32,128]{3,2,1,0:T(8,128)(2,1)S(1)} %get-tuple-element.41), channel_id=1, source_target_pairs={{16,15},{0,31},{48,47},{32,63},{80,79},{64,95},{112,111},{96,127},... | collective-permute-start | bytes 3194888 | tf_op jit(solution)/shard_map/ppermute | solution.py:387
  36.6 10.2 %collective-permute-start.3 = (bf16[25,2,32,128]{3,2,1,0:T(8,128)(2,1)S(1)}, bf16[25,2,32,128]{3,2,1,0:T(8,128)(2,1)S(1)}, u32[]{:S(2)}, u32[]{:S(2)}) collective-permute-start(bf16[25,2,32,128]{3,2,1,0:T(8,128)(2,1)S(1)} %get-tuple-element.34.a.refs_0_), channel_id=1, source_target_pairs={{0,64},{256,320},{32,96},{288,352},{1,65},{257,321},{33,97},{289,3... | collective-permute-start | bytes 1228808 | tf_op jit(solution)/shard_map/ppermute | solution.py:378
  37.9 11.0 %collective-permute-start.4 = (bf16[25,2,32,128]{3,2,1,0:T(8,128)(2,1)S(1)}, bf16[25,2,32,128]{3,2,1,0:T(8,128)(2,1)S(1)}, u32[]{:S(2)}, u32[]{:S(2)}) collective-permute-start(bf16[25,2,32,128]{3,2,1,0:T(8,128)(2,1)S(1)} %get-tuple-element.35.b.refs_1_), channel_id=1, source_target_pairs={{0,192},{256,448},{32,224},{288,480},{1,193},{257,449},{33,225},{2... | collective-permute-start | bytes 1228808 | tf_op jit(solution)/shard_map/ppermute | solution.py:378
  48.9 22.8 %collective-permute-start.10 = (bf16[35,2,32,128]{3,2,1,0:T(8,128)(2,1)S(1)}, bf16[35,2,32,128]{3,2,1,0:T(8,128)(2,1)S(1)}, u32[]{:S(2)}, u32[]{:S(2)}) collective-permute-start(bf16[35,2,32,128]{3,2,1,0:T(8,128)(2,1)S(1)} %collective-permute-done.5), channel_id=1, source_target_pairs={{0,15},{16,31},{32,47},{48,63},{64,79},{80,95},{96,111},{112,127},... | collective-permute-start | bytes 1720328 | tf_op jit(solution)/shard_map/ppermute | solution.py:395
  50.9 10.0 %collective-permute-start.6 = (bf16[25,2,32,128]{3,2,1,0:T(8,128)(2,1)S(1)}, bf16[25,2,32,128]{3,2,1,0:T(8,128)(2,1)S(1)}, u32[]{:S(2)}, u32[]{:S(2)}) collective-permute-start(bf16[25,2,32,128]{3,2,1,0:T(8,128)(2,1)S(1)} %get-tuple-element.39), channel_id=1, source_target_pairs={{0,64},{256,320},{32,96},{288,352},{1,65},{257,321},{33,97},{289,3... | collective-permute-start | bytes 1228808 | tf_op jit(solution)/shard_map/ppermute | solution.py:378
  52.9 12.4 %collective-permute-start.7 = (bf16[25,2,32,128]{3,2,1,0:T(8,128)(2,1)S(1)}, bf16[25,2,32,128]{3,2,1,0:T(8,128)(2,1)S(1)}, u32[]{:S(2)}, u32[]{:S(2)}) collective-permute-start(bf16[25,2,32,128]{3,2,1,0:T(8,128)(2,1)S(1)} %get-tuple-element.40), channel_id=1, source_target_pairs={{0,192},{256,448},{32,224},{288,480},{1,193},{257,449},{33,225},{2... | collective-permute-start | bytes 1228808 | tf_op jit(solution)/shard_map/ppermute | solution.py:378
  72.4 5.9 %collective-permute-start.11 = (bf16[50,2,32,128]{3,2,1,0:T(8,128)(2,1)S(1)}, bf16[50,2,32,128]{3,2,1,0:T(8,128)(2,1)S(1)}, u32[]{:S(2)}, u32[]{:S(2)}) collective-permute-start(bf16[50,2,32,128]{3,2,1,0:T(8,128)(2,1)S(1)} %get-tuple-element.49.left), channel_id=1, source_target_pairs={{0,32},{32,0},{64,96},{96,64},{128,160},{160,128},{192,224},{224,1... | collective-permute-start | bytes 2457608 | tf_op jit(solution)/shard_map/ppermute | solution.py:400

commit v4 on v3

--- a/solution.py
+++ b/solution.py
@@ -388,7 +388,7 @@
     cross = lax.ppermute(cross, "col", [(0, n_z), (n_z, 0)])
     up = send(a, up_0)
     down = send(b, down_0)
-    up, down, cross = lax.optimization_barrier((up, down, cross))
+    up, down = lax.optimization_barrier((up, down))
     c, d = turn(flags, a, b, up, down)
     up_2 = send(c, up_0 + up_1)
     down_2 = send(d, down_0 + down_1)

time: 84.9 us -> 84.2 us (level)
    ppermute x7, waiting for transfers between devices: 24.6 us -> 16 us  [local(): send = lambda v, route: lax.ppermute(v, ('row', 'col'), route)]
    ppermute x1, waiting for transfers between devices: 0.01 us -> 7.35 us  [local(): cross = lax.ppermute(cross, 'col', [(0, n_z), (n_z, 0)])]
    ppermute x1, waiting for transfers between devices: 6.5 us -> 7.82 us  [local(): cross = lax.ppermute(cross, 'col', [(0, n_z - 1), (n_z, n_col - 1)])]
  transfers between devices with their start and end apart: 12 -> 12, of which waited for: 6 -> 5; matrix products, arithmetic and copies ran while one was open for 0% -> 0% of each run, Pallas kernels for 5% -> 5%
where the time goes in v4:
time: 84.2 us; the launch traced here: 84 us
  starting transfers between devices  35.8 us (43%)
  waiting for transfers between devices  31.1 us (37%)
  Pallas kernels  14.4 us (17%)
  local copies, waits for them, and re-layouts  1.8 us (2%)
    ppermute x1, starting transfers between devices, local(): cross = lax.ppermute(cross, 'col', [(0, n_z), (n_z, 0)])  17.1 us
    ppermute x7, waiting for transfers between devices, local(): send = lambda v, route: lax.ppermute(v, ('row', 'col'), route)  16 us
    ppermute x7, starting transfers between devices, local(): send = lambda v, route: lax.ppermute(v, ('row', 'col'), route)  12 us
    pallas_call x2, Pallas kernels, multiply(): pl.pallas_call(functools.partial(multiply_kernel, phase), out_shape=out,...  8.92 us
    ppermute x1, waiting for transfers between devices, local(): cross = lax.ppermute(cross, 'col', [(0, n_z - 1), (n_z, n_col - 1)])  7.82 us
    ppermute x1, waiting for transfers between devices, local(): cross = lax.ppermute(cross, 'col', [(0, n_z), (n_z, 0)])  7.35 us
    pallas_call x1, Pallas kernels, prep(): pl.pallas_call(prep_kernel, out_shape=(jax.ShapeDtypeStruct((2, rows + 2,...  3.52 us
    ppermute x1, starting transfers between devices, local(): other = lax.ppermute(mine, 'row', [(i, i ^ 1) for i in range(n_row)])  2.66 us
  transfers between devices with their start and end apart: 12, of which 5 were waited for; matrix products, arithmetic and copies ran while one was open for 0% of the time, Pallas kernels for 5%

profile of v4, /device:TPU:1, one launch (start us, length us, event | category | flops | bytes accessed | tf_op | source)
XLA Modules:
  0.0 84.0 jit_solution(16620741012228684058)
XLA Ops:
  0.0 0.7 pad_add_fusion.table
  0.8 1.4 %copy-done = bf16[48,4,4096]{2,1,0:T(4,128)(2,1)S(1)} copy-done((bf16[48,4,4096]{2,1,0:T(4,128)(2,1)S(1)}, bf16[48,4,4096]{2,1,0:T(4,128)(2,1)}, u32[]{:S(2)}) %copy-start) | copy-done | bytes 1572888
  2.2 3.5 %prep.1 = (bf16[2,50,2,32,128]{4,3,2,1,0:T(8,128)(2,1)S(1)}, f32[48,128]{1,0:T(8,128)S(1)}) custom-call(s32[6]{0:T(128)S(1)} %stack.35.flags, s32[5,48]{1,0:T(8,128)S(1)} %pad_add_fusion.table, bf16[48,4,4096]{2,1,0:T(4,128)(2,1)S(1)} %copy-done), custom_call_target="tpu_custom_call" | custom-call | tf_op jit(solution)/shard_map/prep/pallas_call | solution.py:75
  6.0 0.7 collective-permute-start
  6.8 1.3 %collective-permute-start.2 = (bf16[50,2,32,128]{3,2,1,0:T(8,128)(2,1)S(1)}, bf16[50,2,32,128]{3,2,1,0:T(8,128)(2,1)S(1)}, u32[]{:S(2)}, u32[]{:S(2)}) collective-permute-start(bf16[50,2,32,128]{3,2,1,0:T(8,128)(2,1)S(1)} %get-tuple-element.51.refs_1_), channel_id=1, source_target_pairs={{0,32},{34,2},{68,100},{102,70},{136,168},{170,138},{204,236},{238... | collective-permute-start | bytes 2457608 | tf_op jit(solution)/shard_map/ppermute | solution.py:378
  8.1 0.7 collective-permute-start.1
  8.8 1.3 %collective-permute-start.7 = (bf16[2,50,2,32,128]{4,3,2,1,0:T(8,128)(2,1)S(1)}, bf16[2,50,2,32,128]{4,3,2,1,0:T(8,128)(2,1)S(1)}, u32[]{:S(2)}, u32[]{:S(2)}) collective-permute-start(bf16[2,50,2,32,128]{4,3,2,1,0:T(8,128)(2,1)S(1)} %get-tuple-element.29.refs_5_.own), channel_id=1, source_target_pairs={{1,0},{2,1},{3,2},{4,3},{5,4},{6,5},{7,6},{8,7},{9,8},{10,9},{11,1... | collective-permute-start | bytes 4915208 | tf_op jit(solution)/shard_map/ppermute | solution.py:381
  10.1 7.3 %collective-permute-done.2.refs_4_ = bf16[50,2,32,128]{3,2,1,0:T(8,128)(2,1)S(1)} collective-permute-done((bf16[50,2,32,128]{3,2,1,0:T(8,128)(2,1)S(1)}, bf16[50,2,32,128]{3,2,1,0:T(8,128)(2,1)S(1)}, u32[]{:S(2)}, u32[]{:S(2)}) %collective-permute-start.2) | collective-permute-done | bytes 819232 | tf_op jit(solution)/shard_map/ppermute | solution.py:378
  17.4 0.7 pick.1
  18.1 17.1 %collective-permute-start.9 = (bf16[35,2,32,128]{3,2,1,0:T(8,128)(2,1)S(1)}, bf16[35,2,32,128]{3,2,1,0:T(8,128)(2,1)S(1)}, u32[]{:S(2)}, u32[]{:S(2)}) collective-permute-start(bf16[35,2,32,128]{3,2,1,0:T(8,128)(2,1)S(1)} %get-tuple-element.40), channel_id=1, source_target_pairs={{0,16},{16,0},{32,48},{48,32},{64,80},{80,64},{96,112},{112,96},{1... | collective-permute-start | bytes 1720328 | tf_op jit(solution)/shard_map/ppermute | solution.py:388
  35.2 1.4 %collective-permute-start.8 = (bf16[65,2,32,128]{3,2,1,0:T(8,128)(2,1)S(1)}, bf16[65,2,32,128]{3,2,1,0:T(8,128)(2,1)S(1)}, u32[]{:S(2)}, u32[]{:S(2)}) collective-permute-start(bf16[65,2,32,128]{3,2,1,0:T(8,128)(2,1)S(1)} %get-tuple-element.39), channel_id=1, source_target_pairs={{16,15},{0,31},{48,47},{32,63},{80,79},{64,95},{112,111},{96,127},... | collective-permute-start | bytes 3194888 | tf_op jit(solution)/shard_map/ppermute | solution.py:387
  36.6 1.3 %collective-permute-start.3 = (bf16[25,2,32,128]{3,2,1,0:T(8,128)(2,1)S(1)}, bf16[25,2,32,128]{3,2,1,0:T(8,128)(2,1)S(1)}, u32[]{:S(2)}, u32[]{:S(2)}) collective-permute-start(bf16[25,2,32,128]{3,2,1,0:T(8,128)(2,1)S(1)} %get-tuple-element.33.a.refs_0_), channel_id=1, source_target_pairs={{0,64},{256,320},{32,96},{288,352},{1,65},{257,321},{33,97},{289,3... | collective-permute-start | bytes 1228808 | tf_op jit(solution)/shard_map/ppermute | solution.py:378
  37.9 2.4 %collective-permute-start.4 = (bf16[25,2,32,128]{3,2,1,0:T(8,128)(2,1)S(1)}, bf16[25,2,32,128]{3,2,1,0:T(8,128)(2,1)S(1)}, u32[]{:S(2)}, u32[]{:S(2)}) collective-permute-start(bf16[25,2,32,128]{3,2,1,0:T(8,128)(2,1)S(1)} %get-tuple-element.34.b.refs_1_), channel_id=1, source_target_pairs={{0,192},{256,448},{32,224},{288,480},{1,193},{257,449},{33,225},{2... | collective-permute-start | bytes 1228808 | tf_op jit(solution)/shard_map/ppermute | solution.py:378
  40.3 7.4 %collective-permute-done.9 = bf16[35,2,32,128]{3,2,1,0:T(8,128)(2,1)S(1)} collective-permute-done((bf16[35,2,32,128]{3,2,1,0:T(8,128)(2,1)S(1)}, bf16[35,2,32,128]{3,2,1,0:T(8,128)(2,1)S(1)}, u32[]{:S(2)}, u32[]{:S(2)}) %collective-permute-start.9) | collective-permute-done | bytes 573472 | tf_op jit(solution)/shard_map/ppermute | solution.py:388
  47.7 1.3 %collective-permute-start.10 = (bf16[35,2,32,128]{3,2,1,0:T(8,128)(2,1)S(1)}, bf16[35,2,32,128]{3,2,1,0:T(8,128)(2,1)S(1)}, u32[]{:S(2)}, u32[]{:S(2)}) collective-permute-start(bf16[35,2,32,128]{3,2,1,0:T(8,128)(2,1)S(1)} %collective-permute-done.9), channel_id=1, source_target_pairs={{0,15},{16,31},{32,47},{48,63},{64,79},{80,95},{96,111},{112,127},... | collective-permute-start | bytes 1720328 | tf_op jit(solution)/shard_map/ppermute | solution.py:395
  49.6 1.9 %collective-permute-start.5 = (bf16[25,2,32,128]{3,2,1,0:T(8,128)(2,1)S(1)}, bf16[25,2,32,128]{3,2,1,0:T(8,128)(2,1)S(1)}, u32[]{:S(2)}, u32[]{:S(2)}) collective-permute-start(bf16[25,2,32,128]{3,2,1,0:T(8,128)(2,1)S(1)} %get-tuple-element.37), channel_id=1, source_target_pairs={{0,64},{256,320},{32,96},{288,352},{1,65},{257,321},{33,97},{289,3... | collective-permute-start | bytes 1228808 | tf_op jit(solution)/shard_map/ppermute | solution.py:378
  51.5 3.7 %collective-permute-start.6 = (bf16[25,2,32,128]{3,2,1,0:T(8,128)(2,1)S(1)}, bf16[25,2,32,128]{3,2,1,0:T(8,128)(2,1)S(1)}, u32[]{:S(2)}, u32[]{:S(2)}) collective-permute-start(bf16[25,2,32,128]{3,2,1,0:T(8,128)(2,1)S(1)} %get-tuple-element.38), channel_id=1, source_target_pairs={{0,192},{256,448},{32,224},{288,480},{1,193},{257,449},{33,225},{2... | collective-permute-start | bytes 1228808 | tf_op jit(solution)/shard_map/ppermute | solution.py:378
  55.3 4.3 %collective-permute-done.5.refs_3_.refs_4_ = bf16[25,2,32,128]{3,2,1,0:T(8,128)(2,1)S(1)} collective-permute-done((bf16[25,2,32,128]{3,2,1,0:T(8,128)(2,1)S(1)}, bf16[25,2,32,128]{3,2,1,0:T(8,128)(2,1)S(1)}, u32[]{:S(2)}, u32[]{:S(2)}) %collective-permute-start.5) | collective-permute-done | bytes 409632 | tf_op jit(solution)/shard_map/ppermute | solution.py:378
  59.5 4.4 %collective-permute-done.6.refs_5_.refs_6_ = bf16[25,2,32,128]{3,2,1,0:T(8,128)(2,1)S(1)} collective-permute-done((bf16[25,2,32,128]{3,2,1,0:T(8,128)(2,1)S(1)}, bf16[25,2,32,128]{3,2,1,0:T(8,128)(2,1)S(1)}, u32[]{:S(2)}, u32[]{:S(2)}) %collective-permute-start.6) | collective-permute-done | bytes 409632 | tf_op jit(solution)/shard_map/ppermute | solution.py:378
  64.0 7.8 %collective-permute-done.10.refs_9_ = bf16[35,2,32,128]{3,2,1,0:T(8,128)(2,1)S(1)} collective-permute-done((bf16[35,2,32,128]{3,2,1,0:T(8,128)(2,1)S(1)}, bf16[35,2,32,128]{3,2,1,0:T(8,128)(2,1)S(1)}, u32[]{:S(2)}, u32[]{:S(2)}) %collective-permute-start.10) | collective-permute-done | bytes 573472 | tf_op jit(solution)/shard_map/ppermute | solution.py:395
  71.8 0.6 join.1
  72.4 2.7 %collective-permute-start.11 = (bf16[50,2,32,128]{3,2,1,0:T(8,128)(2,1)S(1)}, bf16[50,2,32,128]{3,2,1,0:T(8,128)(2,1)S(1)}, u32[]{:S(2)}, u32[]{:S(2)}) collective-permute-start(bf16[50,2,32,128]{3,2,1,0:T(8,128)(2,1)S(1)} %get-tuple-element.47.left), channel_id=1, source_target_pairs={{0,32},{32,0},{64,96},{96,64},{128,160},{160,128},{192,224},{224,1... | collective-permute-start | bytes 2457608 | tf_op jit(solution)/shard_map/ppermute | solution.py:400
  75.1 3.2 %multiply0.1 = (f32[49,128,128]{2,1,0:T(8,128)S(1)}, f32[48,128]{1,0:T(8,128)S(1)}) custom-call(s32[6]{0:T(128)S(1)} %stack.35.flags, f32[48,128]{1,0:T(8,128)S(1)} %get-tuple-element.28.om_ref, bf16[2,50,2,32,128]{4,3,2,1,0:T(8,128)(2,1)S(1)} %get-tuple-element.29.refs_5_.own, bf16[2,50,2,32,128]{4,3,2,1,0:T(8,128)(2,1)S(1)} %get-tuple-element.46.behind, ...), custom_call_target="tpu_custom_call" | custom-call | flops 1000000000 | bytes 4194304 | tf_op jit(solution)/shard_map/multiply0/pallas_call | solution.py:311
  78.3 5.8 %multiply1.1 = (bf16[48,4,4096]{2,1,0:T(4,128)(2,1)}, f32[49,128,128]{2,1,0:T(8,128)S(1)}) custom-call(s32[6]{0:T(128)S(1)} %stack.35.flags, f32[48,128]{1,0:T(8,128)S(1)} %get-tuple-element.28.om_ref, bf16[2,50,2,32,128]{4,3,2,1,0:T(8,128)(2,1)S(1)} %get-tuple-element.29.refs_5_.own, ...), custom_call_target="tpu_custom_call", output_to_operand_aliasing={{1}: (6, {})} | custom-call | flops 1000000000 | bytes 4194304 | tf_op jit(solution)/shard_map/multiply1/pallas_call | solution.py:311
  (11 shorter events, 1.0 us)
Async XLA Ops:
  0.8 1.4 %copy-start = (bf16[48,4,4096]{2,1,0:T(4,128)(2,1)S(1)}, bf16[48,4,4096]{2,1,0:T(4,128)(2,1)}, u32[]{:S(2)}) copy-start(bf16[48,4,4096]{2,1,0:T(4,128)(2,1)} %tile.1) | copy-start | bytes 4718596
  6.0 4.0 %collective-permute-start = (bf16[50,2,32,128]{3,2,1,0:T(8,128)(2,1)S(1)}, bf16[50,2,32,128]{3,2,1,0:T(8,128)(2,1)S(1)}, u32[]{:S(2)}, u32[]{:S(2)}) collective-permute-start(bf16[50,2,32,128]{3,2,1,0:T(8,128)(2,1)S(1)} %get-tuple-element.52.refs_0_), channel_id=1, source_target_pairs={{0,256},{1,257},{34,290},{35,291},{68,324},{69,325},{102,358},{103... | collective-permute-start | bytes 2457608 | tf_op jit(solution)/shard_map/ppermute | solution.py:378
  6.8 10.6 %collective-permute-start.2 = (bf16[50,2,32,128]{3,2,1,0:T(8,128)(2,1)S(1)}, bf16[50,2,32,128]{3,2,1,0:T(8,128)(2,1)S(1)}, u32[]{:S(2)}, u32[]{:S(2)}) collective-permute-start(bf16[50,2,32,128]{3,2,1,0:T(8,128)(2,1)S(1)} %get-tuple-element.51.refs_1_), channel_id=1, source_target_pairs={{0,32},{34,2},{68,100},{102,70},{136,168},{170,138},{204,236},{238... | collective-permute-start | bytes 2457608 | tf_op jit(solution)/shard_map/ppermute | solution.py:378
  8.1 9.3 %collective-permute-start.1 = (bf16[50,2,32,128]{3,2,1,0:T(8,128)(2,1)S(1)}, bf16[50,2,32,128]{3,2,1,0:T(8,128)(2,1)S(1)}, u32[]{:S(2)}, u32[]{:S(2)}) collective-permute-start(bf16[50,2,32,128]{3,2,1,0:T(8,128)(2,1)S(1)} %get-tuple-element.51.refs_1_), channel_id=1, source_target_pairs={{0,288},{33,289},{34,258},{67,323},{68,356},{101,357},{102,326},{1... | collective-permute-start | bytes 2457608 | tf_op jit(solution)/shard_map/ppermute | solution.py:378
  8.8 55.2 %collective-permute-start.7 = (bf16[2,50,2,32,128]{4,3,2,1,0:T(8,128)(2,1)S(1)}, bf16[2,50,2,32,128]{4,3,2,1,0:T(8,128)(2,1)S(1)}, u32[]{:S(2)}, u32[]{:S(2)}) collective-permute-start(bf16[2,50,2,32,128]{4,3,2,1,0:T(8,128)(2,1)S(1)} %get-tuple-element.29.refs_5_.own), channel_id=1, source_target_pairs={{1,0},{2,1},{3,2},{4,3},{5,4},{6,5},{7,6},{8,7},{9,8},{10,9},{11,1... | collective-permute-start | bytes 4915208 | tf_op jit(solution)/shard_map/ppermute | solution.py:381
  18.1 29.5 %collective-permute-start.9 = (bf16[35,2,32,128]{3,2,1,0:T(8,128)(2,1)S(1)}, bf16[35,2,32,128]{3,2,1,0:T(8,128)(2,1)S(1)}, u32[]{:S(2)}, u32[]{:S(2)}) collective-permute-start(bf16[35,2,32,128]{3,2,1,0:T(8,128)(2,1)S(1)} %get-tuple-element.40), channel_id=1, source_target_pairs={{0,16},{16,0},{32,48},{48,32},{64,80},{80,64},{96,112},{112,96},{1... | collective-permute-start | bytes 1720328 | tf_op jit(solution)/shard_map/ppermute | solution.py:388
  35.2 28.7 %collective-permute-start.8 = (bf16[65,2,32,128]{3,2,1,0:T(8,128)(2,1)S(1)}, bf16[65,2,32,128]{3,2,1,0:T(8,128)(2,1)S(1)}, u32[]{:S(2)}, u32[]{:S(2)}) collective-permute-start(bf16[65,2,32,128]{3,2,1,0:T(8,128)(2,1)S(1)} %get-tuple-element.39), channel_id=1, source_target_pairs={{16,15},{0,31},{48,47},{32,63},{80,79},{64,95},{112,111},{96,127},... | collective-permute-start | bytes 3194888 | tf_op jit(solution)/shard_map/ppermute | solution.py:387
  36.6 12.4 %collective-permute-start.3 = (bf16[25,2,32,128]{3,2,1,0:T(8,128)(2,1)S(1)}, bf16[25,2,32,128]{3,2,1,0:T(8,128)(2,1)S(1)}, u32[]{:S(2)}, u32[]{:S(2)}) collective-permute-start(bf16[25,2,32,128]{3,2,1,0:T(8,128)(2,1)S(1)} %get-tuple-element.33.a.refs_0_), channel_id=1, source_target_pairs={{0,64},{256,320},{32,96},{288,352},{1,65},{257,321},{33,97},{289,3... | collective-permute-start | bytes 1228808 | tf_op jit(solution)/shard_map/ppermute | solution.py:378
  37.9 11.1 %collective-permute-start.4 = (bf16[25,2,32,128]{3,2,1,0:T(8,128)(2,1)S(1)}, bf16[25,2,32,128]{3,2,1,0:T(8,128)(2,1)S(1)}, u32[]{:S(2)}, u32[]{:S(2)}) collective-permute-start(bf16[25,2,32,128]{3,2,1,0:T(8,128)(2,1)S(1)} %get-tuple-element.34.b.refs_1_), channel_id=1, source_target_pairs={{0,192},{256,448},{32,224},{288,480},{1,193},{257,449},{33,225},{2... | collective-permute-start | bytes 1228808 | tf_op jit(solution)/shard_map/ppermute | solution.py:378
  47.7 24.1 %collective-permute-start.10 = (bf16[35,2,32,128]{3,2,1,0:T(8,128)(2,1)S(1)}, bf16[35,2,32,128]{3,2,1,0:T(8,128)(2,1)S(1)}, u32[]{:S(2)}, u32[]{:S(2)}) collective-permute-start(bf16[35,2,32,128]{3,2,1,0:T(8,128)(2,1)S(1)} %collective-permute-done.9), channel_id=1, source_target_pairs={{0,15},{16,31},{32,47},{48,63},{64,79},{80,95},{96,111},{112,127},... | collective-permute-start | bytes 1720328 | tf_op jit(solution)/shard_map/ppermute | solution.py:395
  49.6 9.9 %collective-permute-start.5 = (bf16[25,2,32,128]{3,2,1,0:T(8,128)(2,1)S(1)}, bf16[25,2,32,128]{3,2,1,0:T(8,128)(2,1)S(1)}, u32[]{:S(2)}, u32[]{:S(2)}) collective-permute-start(bf16[25,2,32,128]{3,2,1,0:T(8,128)(2,1)S(1)} %get-tuple-element.37), channel_id=1, source_target_pairs={{0,64},{256,320},{32,96},{288,352},{1,65},{257,321},{33,97},{289,3... | collective-permute-start | bytes 1228808 | tf_op jit(solution)/shard_map/ppermute | solution.py:378
  51.5 12.4 %collective-permute-start.6 = (bf16[25,2,32,128]{3,2,1,0:T(8,128)(2,1)S(1)}, bf16[25,2,32,128]{3,2,1,0:T(8,128)(2,1)S(1)}, u32[]{:S(2)}, u32[]{:S(2)}) collective-permute-start(bf16[25,2,32,128]{3,2,1,0:T(8,128)(2,1)S(1)} %get-tuple-element.38), channel_id=1, source_target_pairs={{0,192},{256,448},{32,224},{288,480},{1,193},{257,449},{33,225},{2... | collective-permute-start | bytes 1228808 | tf_op jit(solution)/shard_map/ppermute | solution.py:378
  72.4 5.8 %collective-permute-start.11 = (bf16[50,2,32,128]{3,2,1,0:T(8,128)(2,1)S(1)}, bf16[50,2,32,128]{3,2,1,0:T(8,128)(2,1)S(1)}, u32[]{:S(2)}, u32[]{:S(2)}) collective-permute-start(bf16[50,2,32,128]{3,2,1,0:T(8,128)(2,1)S(1)} %get-tuple-element.47.left), channel_id=1, source_target_pairs={{0,32},{32,0},{64,96},{96,64},{128,160},{160,128},{192,224},{224,1... | collective-permute-start | bytes 2457608 | tf_op jit(solution)/shard_map/ppermute | solution.py:400

commit v5 on v4

--- a/solution.py
+++ b/solution.py
@@ -10,7 +10,7 @@
 HALF = 2
 SUB = 32
 LANES = 128
-AHEAD = 6
+AHEAD = 8
 FIRST, WHICH, ROLE, HEAD, LAST, SECTION = range(6)
 CROSS = 35
 LEFT = 32

time: 84.2 us -> 83.8 us (level)
  no operation moved by 1% of the time
where the time goes in v5:
time: 83.8 us; the launch traced here: 83.5 us
  starting transfers between devices  35.8 us (43%)
  waiting for transfers between devices  31.1 us (37%)
  Pallas kernels  13.9 us (17%)
  local copies, waits for them, and re-layouts  1.8 us (2%)
    ppermute x1, starting transfers between devices, local(): cross = lax.ppermute(cross, 'col', [(0, n_z), (n_z, 0)])  17.1 us
    ppermute x7, waiting for transfers between devices, local(): send = lambda v, route: lax.ppermute(v, ('row', 'col'), route)  16 us
    ppermute x7, starting transfers between devices, local(): send = lambda v, route: lax.ppermute(v, ('row', 'col'), route)  12 us
    pallas_call x2, Pallas kernels, multiply(): pl.pallas_call(functools.partial(multiply_kernel, phase), out_shape=out,...  8.37 us
    ppermute x1, waiting for transfers between devices, local(): cross = lax.ppermute(cross, 'col', [(0, n_z - 1), (n_z, n_col - 1)])  7.82 us
    ppermute x1, waiting for transfers between devices, local(): cross = lax.ppermute(cross, 'col', [(0, n_z), (n_z, 0)])  7.35 us
    pallas_call x1, Pallas kernels, prep(): pl.pallas_call(prep_kernel, out_shape=(jax.ShapeDtypeStruct((2, rows + 2,...  3.52 us
    ppermute x1, starting transfers between devices, local(): other = lax.ppermute(mine, 'row', [(i, i ^ 1) for i in range(n_row)])  2.66 us
  transfers between devices with their start and end apart: 12, of which 5 were waited for; matrix products, arithmetic and copies ran while one was open for 0% of the time, Pallas kernels for 5%

profile of v5, /device:TPU:1, one launch (start us, length us, event | category | flops | bytes accessed | tf_op | source)
XLA Modules:
  0.0 83.5 jit_solution(15634568861737818236)
XLA Ops:
  0.0 0.7 pad_add_fusion.table
  0.8 1.4 %copy-done = bf16[48,4,4096]{2,1,0:T(4,128)(2,1)S(1)} copy-done((bf16[48,4,4096]{2,1,0:T(4,128)(2,1)S(1)}, bf16[48,4,4096]{2,1,0:T(4,128)(2,1)}, u32[]{:S(2)}) %copy-start) | copy-done | bytes 1572888
  2.2 3.5 %prep.1 = (bf16[2,50,2,32,128]{4,3,2,1,0:T(8,128)(2,1)S(1)}, f32[48,128]{1,0:T(8,128)S(1)}) custom-call(s32[6]{0:T(128)S(1)} %stack.35.flags, s32[5,48]{1,0:T(8,128)S(1)} %pad_add_fusion.table, bf16[48,4,4096]{2,1,0:T(4,128)(2,1)S(1)} %copy-done), custom_call_target="tpu_custom_call" | custom-call | tf_op jit(solution)/shard_map/prep/pallas_call | solution.py:75
  6.0 0.7 collective-permute-start
  6.8 1.3 %collective-permute-start.2 = (bf16[50,2,32,128]{3,2,1,0:T(8,128)(2,1)S(1)}, bf16[50,2,32,128]{3,2,1,0:T(8,128)(2,1)S(1)}, u32[]{:S(2)}, u32[]{:S(2)}) collective-permute-start(bf16[50,2,32,128]{3,2,1,0:T(8,128)(2,1)S(1)} %get-tuple-element.51.refs_1_), channel_id=1, source_target_pairs={{0,32},{34,2},{68,100},{102,70},{136,168},{170,138},{204,236},{238... | collective-permute-start | bytes 2457608 | tf_op jit(solution)/shard_map/ppermute | solution.py:378
  8.1 0.7 collective-permute-start.1
  8.8 1.3 %collective-permute-start.7 = (bf16[2,50,2,32,128]{4,3,2,1,0:T(8,128)(2,1)S(1)}, bf16[2,50,2,32,128]{4,3,2,1,0:T(8,128)(2,1)S(1)}, u32[]{:S(2)}, u32[]{:S(2)}) collective-permute-start(bf16[2,50,2,32,128]{4,3,2,1,0:T(8,128)(2,1)S(1)} %get-tuple-element.29.refs_5_.own), channel_id=1, source_target_pairs={{1,0},{2,1},{3,2},{4,3},{5,4},{6,5},{7,6},{8,7},{9,8},{10,9},{11,1... | collective-permute-start | bytes 4915208 | tf_op jit(solution)/shard_map/ppermute | solution.py:381
  10.1 7.3 %collective-permute-done.2.refs_4_ = bf16[50,2,32,128]{3,2,1,0:T(8,128)(2,1)S(1)} collective-permute-done((bf16[50,2,32,128]{3,2,1,0:T(8,128)(2,1)S(1)}, bf16[50,2,32,128]{3,2,1,0:T(8,128)(2,1)S(1)}, u32[]{:S(2)}, u32[]{:S(2)}) %collective-permute-start.2) | collective-permute-done | bytes 819232 | tf_op jit(solution)/shard_map/ppermute | solution.py:378
  17.4 0.7 pick.1
  18.1 17.1 %collective-permute-start.9 = (bf16[35,2,32,128]{3,2,1,0:T(8,128)(2,1)S(1)}, bf16[35,2,32,128]{3,2,1,0:T(8,128)(2,1)S(1)}, u32[]{:S(2)}, u32[]{:S(2)}) collective-permute-start(bf16[35,2,32,128]{3,2,1,0:T(8,128)(2,1)S(1)} %get-tuple-element.40), channel_id=1, source_target_pairs={{0,16},{16,0},{32,48},{48,32},{64,80},{80,64},{96,112},{112,96},{1... | collective-permute-start | bytes 1720328 | tf_op jit(solution)/shard_map/ppermute | solution.py:388
  35.2 1.4 %collective-permute-start.8 = (bf16[65,2,32,128]{3,2,1,0:T(8,128)(2,1)S(1)}, bf16[65,2,32,128]{3,2,1,0:T(8,128)(2,1)S(1)}, u32[]{:S(2)}, u32[]{:S(2)}) collective-permute-start(bf16[65,2,32,128]{3,2,1,0:T(8,128)(2,1)S(1)} %get-tuple-element.39), channel_id=1, source_target_pairs={{16,15},{0,31},{48,47},{32,63},{80,79},{64,95},{112,111},{96,127},... | collective-permute-start | bytes 3194888 | tf_op jit(solution)/shard_map/ppermute | solution.py:387
  36.6 1.3 %collective-permute-start.3 = (bf16[25,2,32,128]{3,2,1,0:T(8,128)(2,1)S(1)}, bf16[25,2,32,128]{3,2,1,0:T(8,128)(2,1)S(1)}, u32[]{:S(2)}, u32[]{:S(2)}) collective-permute-start(bf16[25,2,32,128]{3,2,1,0:T(8,128)(2,1)S(1)} %get-tuple-element.33.a.refs_0_), channel_id=1, source_target_pairs={{0,64},{256,320},{32,96},{288,352},{1,65},{257,321},{33,97},{289,3... | collective-permute-start | bytes 1228808 | tf_op jit(solution)/shard_map/ppermute | solution.py:378
  37.9 2.4 %collective-permute-start.4 = (bf16[25,2,32,128]{3,2,1,0:T(8,128)(2,1)S(1)}, bf16[25,2,32,128]{3,2,1,0:T(8,128)(2,1)S(1)}, u32[]{:S(2)}, u32[]{:S(2)}) collective-permute-start(bf16[25,2,32,128]{3,2,1,0:T(8,128)(2,1)S(1)} %get-tuple-element.34.b.refs_1_), channel_id=1, source_target_pairs={{0,192},{256,448},{32,224},{288,480},{1,193},{257,449},{33,225},{2... | collective-permute-start | bytes 1228808 | tf_op jit(solution)/shard_map/ppermute | solution.py:378
  40.3 7.4 %collective-permute-done.9 = bf16[35,2,32,128]{3,2,1,0:T(8,128)(2,1)S(1)} collective-permute-done((bf16[35,2,32,128]{3,2,1,0:T(8,128)(2,1)S(1)}, bf16[35,2,32,128]{3,2,1,0:T(8,128)(2,1)S(1)}, u32[]{:S(2)}, u32[]{:S(2)}) %collective-permute-start.9) | collective-permute-done | bytes 573472 | tf_op jit(solution)/shard_map/ppermute | solution.py:388
  47.7 1.3 %collective-permute-start.10 = (bf16[35,2,32,128]{3,2,1,0:T(8,128)(2,1)S(1)}, bf16[35,2,32,128]{3,2,1,0:T(8,128)(2,1)S(1)}, u32[]{:S(2)}, u32[]{:S(2)}) collective-permute-start(bf16[35,2,32,128]{3,2,1,0:T(8,128)(2,1)S(1)} %collective-permute-done.9), channel_id=1, source_target_pairs={{0,15},{16,31},{32,47},{48,63},{64,79},{80,95},{96,111},{112,127},... | collective-permute-start | bytes 1720328 | tf_op jit(solution)/shard_map/ppermute | solution.py:395
  49.6 1.9 %collective-permute-start.5 = (bf16[25,2,32,128]{3,2,1,0:T(8,128)(2,1)S(1)}, bf16[25,2,32,128]{3,2,1,0:T(8,128)(2,1)S(1)}, u32[]{:S(2)}, u32[]{:S(2)}) collective-permute-start(bf16[25,2,32,128]{3,2,1,0:T(8,128)(2,1)S(1)} %get-tuple-element.37), channel_id=1, source_target_pairs={{0,64},{256,320},{32,96},{288,352},{1,65},{257,321},{33,97},{289,3... | collective-permute-start | bytes 1228808 | tf_op jit(solution)/shard_map/ppermute | solution.py:378
  51.5 3.7 %collective-permute-start.6 = (bf16[25,2,32,128]{3,2,1,0:T(8,128)(2,1)S(1)}, bf16[25,2,32,128]{3,2,1,0:T(8,128)(2,1)S(1)}, u32[]{:S(2)}, u32[]{:S(2)}) collective-permute-start(bf16[25,2,32,128]{3,2,1,0:T(8,128)(2,1)S(1)} %get-tuple-element.38), channel_id=1, source_target_pairs={{0,192},{256,448},{32,224},{288,480},{1,193},{257,449},{33,225},{2... | collective-permute-start | bytes 1228808 | tf_op jit(solution)/shard_map/ppermute | solution.py:378
  55.3 4.3 %collective-permute-done.5.refs_3_.refs_4_ = bf16[25,2,32,128]{3,2,1,0:T(8,128)(2,1)S(1)} collective-permute-done((bf16[25,2,32,128]{3,2,1,0:T(8,128)(2,1)S(1)}, bf16[25,2,32,128]{3,2,1,0:T(8,128)(2,1)S(1)}, u32[]{:S(2)}, u32[]{:S(2)}) %collective-permute-start.5) | collective-permute-done | bytes 409632 | tf_op jit(solution)/shard_map/ppermute | solution.py:378
  59.5 4.4 %collective-permute-done.6.refs_5_.refs_6_ = bf16[25,2,32,128]{3,2,1,0:T(8,128)(2,1)S(1)} collective-permute-done((bf16[25,2,32,128]{3,2,1,0:T(8,128)(2,1)S(1)}, bf16[25,2,32,128]{3,2,1,0:T(8,128)(2,1)S(1)}, u32[]{:S(2)}, u32[]{:S(2)}) %collective-permute-start.6) | collective-permute-done | bytes 409632 | tf_op jit(solution)/shard_map/ppermute | solution.py:378
  64.0 7.8 %collective-permute-done.10.refs_9_ = bf16[35,2,32,128]{3,2,1,0:T(8,128)(2,1)S(1)} collective-permute-done((bf16[35,2,32,128]{3,2,1,0:T(8,128)(2,1)S(1)}, bf16[35,2,32,128]{3,2,1,0:T(8,128)(2,1)S(1)}, u32[]{:S(2)}, u32[]{:S(2)}) %collective-permute-start.10) | collective-permute-done | bytes 573472 | tf_op jit(solution)/shard_map/ppermute | solution.py:395
  71.8 0.6 join.1
  72.4 2.7 %collective-permute-start.11 = (bf16[50,2,32,128]{3,2,1,0:T(8,128)(2,1)S(1)}, bf16[50,2,32,128]{3,2,1,0:T(8,128)(2,1)S(1)}, u32[]{:S(2)}, u32[]{:S(2)}) collective-permute-start(bf16[50,2,32,128]{3,2,1,0:T(8,128)(2,1)S(1)} %get-tuple-element.47.left), channel_id=1, source_target_pairs={{0,32},{32,0},{64,96},{96,64},{128,160},{160,128},{192,224},{224,1... | collective-permute-start | bytes 2457608 | tf_op jit(solution)/shard_map/ppermute | solution.py:400
  75.1 2.8 %multiply0.1 = (f32[49,128,128]{2,1,0:T(8,128)S(1)}, f32[48,128]{1,0:T(8,128)S(1)}) custom-call(s32[6]{0:T(128)S(1)} %stack.35.flags, f32[48,128]{1,0:T(8,128)S(1)} %get-tuple-element.28.om_ref, bf16[2,50,2,32,128]{4,3,2,1,0:T(8,128)(2,1)S(1)} %get-tuple-element.29.refs_5_.own, bf16[2,50,2,32,128]{4,3,2,1,0:T(8,128)(2,1)S(1)} %get-tuple-element.46.behind, ...), custom_call_target="tpu_custom_call" | custom-call | flops 1000000000 | bytes 4194304 | tf_op jit(solution)/shard_map/multiply0/pallas_call | solution.py:311
  77.9 5.5 %multiply1.1 = (bf16[48,4,4096]{2,1,0:T(4,128)(2,1)}, f32[49,128,128]{2,1,0:T(8,128)S(1)}) custom-call(s32[6]{0:T(128)S(1)} %stack.35.flags, f32[48,128]{1,0:T(8,128)S(1)} %get-tuple-element.28.om_ref, bf16[2,50,2,32,128]{4,3,2,1,0:T(8,128)(2,1)S(1)} %get-tuple-element.29.refs_5_.own, ...), custom_call_target="tpu_custom_call", output_to_operand_aliasing={{1}: (6, {})} | custom-call | flops 1000000000 | bytes 4194304 | tf_op jit(solution)/shard_map/multiply1/pallas_call | solution.py:311
  (11 shorter events, 1.0 us)
Async XLA Ops:
  0.8 1.4 %copy-start = (bf16[48,4,4096]{2,1,0:T(4,128)(2,1)S(1)}, bf16[48,4,4096]{2,1,0:T(4,128)(2,1)}, u32[]{:S(2)}) copy-start(bf16[48,4,4096]{2,1,0:T(4,128)(2,1)} %tile.1) | copy-start | bytes 4718596
  6.0 4.0 %collective-permute-start = (bf16[50,2,32,128]{3,2,1,0:T(8,128)(2,1)S(1)}, bf16[50,2,32,128]{3,2,1,0:T(8,128)(2,1)S(1)}, u32[]{:S(2)}, u32[]{:S(2)}) collective-permute-start(bf16[50,2,32,128]{3,2,1,0:T(8,128)(2,1)S(1)} %get-tuple-element.52.refs_0_), channel_id=1, source_target_pairs={{0,256},{1,257},{34,290},{35,291},{68,324},{69,325},{102,358},{103... | collective-permute-start | bytes 2457608 | tf_op jit(solution)/shard_map/ppermute | solution.py:378
  6.8 10.6 %collective-permute-start.2 = (bf16[50,2,32,128]{3,2,1,0:T(8,128)(2,1)S(1)}, bf16[50,2,32,128]{3,2,1,0:T(8,128)(2,1)S(1)}, u32[]{:S(2)}, u32[]{:S(2)}) collective-permute-start(bf16[50,2,32,128]{3,2,1,0:T(8,128)(2,1)S(1)} %get-tuple-element.51.refs_1_), channel_id=1, source_target_pairs={{0,32},{34,2},{68,100},{102,70},{136,168},{170,138},{204,236},{238... | collective-permute-start | bytes 2457608 | tf_op jit(solution)/shard_map/ppermute | solution.py:378
  8.1 9.3 %collective-permute-start.1 = (bf16[50,2,32,128]{3,2,1,0:T(8,128)(2,1)S(1)}, bf16[50,2,32,128]{3,2,1,0:T(8,128)(2,1)S(1)}, u32[]{:S(2)}, u32[]{:S(2)}) collective-permute-start(bf16[50,2,32,128]{3,2,1,0:T(8,128)(2,1)S(1)} %get-tuple-element.51.refs_1_), channel_id=1, source_target_pairs={{0,288},{33,289},{34,258},{67,323},{68,356},{101,357},{102,326},{1... | collective-permute-start | bytes 2457608 | tf_op jit(solution)/shard_map/ppermute | solution.py:378
  8.8 55.2 %collective-permute-start.7 = (bf16[2,50,2,32,128]{4,3,2,1,0:T(8,128)(2,1)S(1)}, bf16[2,50,2,32,128]{4,3,2,1,0:T(8,128)(2,1)S(1)}, u32[]{:S(2)}, u32[]{:S(2)}) collective-permute-start(bf16[2,50,2,32,128]{4,3,2,1,0:T(8,128)(2,1)S(1)} %get-tuple-element.29.refs_5_.own), channel_id=1, source_target_pairs={{1,0},{2,1},{3,2},{4,3},{5,4},{6,5},{7,6},{8,7},{9,8},{10,9},{11,1... | collective-permute-start | bytes 4915208 | tf_op jit(solution)/shard_map/ppermute | solution.py:381
  18.1 29.5 %collective-permute-start.9 = (bf16[35,2,32,128]{3,2,1,0:T(8,128)(2,1)S(1)}, bf16[35,2,32,128]{3,2,1,0:T(8,128)(2,1)S(1)}, u32[]{:S(2)}, u32[]{:S(2)}) collective-permute-start(bf16[35,2,32,128]{3,2,1,0:T(8,128)(2,1)S(1)} %get-tuple-element.40), channel_id=1, source_target_pairs={{0,16},{16,0},{32,48},{48,32},{64,80},{80,64},{96,112},{112,96},{1... | collective-permute-start | bytes 1720328 | tf_op jit(solution)/shard_map/ppermute | solution.py:388
  35.2 28.7 %collective-permute-start.8 = (bf16[65,2,32,128]{3,2,1,0:T(8,128)(2,1)S(1)}, bf16[65,2,32,128]{3,2,1,0:T(8,128)(2,1)S(1)}, u32[]{:S(2)}, u32[]{:S(2)}) collective-permute-start(bf16[65,2,32,128]{3,2,1,0:T(8,128)(2,1)S(1)} %get-tuple-element.39), channel_id=1, source_target_pairs={{16,15},{0,31},{48,47},{32,63},{80,79},{64,95},{112,111},{96,127},... | collective-permute-start | bytes 3194888 | tf_op jit(solution)/shard_map/ppermute | solution.py:387
  36.6 12.4 %collective-permute-start.3 = (bf16[25,2,32,128]{3,2,1,0:T(8,128)(2,1)S(1)}, bf16[25,2,32,128]{3,2,1,0:T(8,128)(2,1)S(1)}, u32[]{:S(2)}, u32[]{:S(2)}) collective-permute-start(bf16[25,2,32,128]{3,2,1,0:T(8,128)(2,1)S(1)} %get-tuple-element.33.a.refs_0_), channel_id=1, source_target_pairs={{0,64},{256,320},{32,96},{288,352},{1,65},{257,321},{33,97},{289,3... | collective-permute-start | bytes 1228808 | tf_op jit(solution)/shard_map/ppermute | solution.py:378
  37.9 11.1 %collective-permute-start.4 = (bf16[25,2,32,128]{3,2,1,0:T(8,128)(2,1)S(1)}, bf16[25,2,32,128]{3,2,1,0:T(8,128)(2,1)S(1)}, u32[]{:S(2)}, u32[]{:S(2)}) collective-permute-start(bf16[25,2,32,128]{3,2,1,0:T(8,128)(2,1)S(1)} %get-tuple-element.34.b.refs_1_), channel_id=1, source_target_pairs={{0,192},{256,448},{32,224},{288,480},{1,193},{257,449},{33,225},{2... | collective-permute-start | bytes 1228808 | tf_op jit(solution)/shard_map/ppermute | solution.py:378
  47.7 24.1 %collective-permute-start.10 = (bf16[35,2,32,128]{3,2,1,0:T(8,128)(2,1)S(1)}, bf16[35,2,32,128]{3,2,1,0:T(8,128)(2,1)S(1)}, u32[]{:S(2)}, u32[]{:S(2)}) collective-permute-start(bf16[35,2,32,128]{3,2,1,0:T(8,128)(2,1)S(1)} %collective-permute-done.9), channel_id=1, source_target_pairs={{0,15},{16,31},{32,47},{48,63},{64,79},{80,95},{96,111},{112,127},... | collective-permute-start | bytes 1720328 | tf_op jit(solution)/shard_map/ppermute | solution.py:395
  49.6 9.9 %collective-permute-start.5 = (bf16[25,2,32,128]{3,2,1,0:T(8,128)(2,1)S(1)}, bf16[25,2,32,128]{3,2,1,0:T(8,128)(2,1)S(1)}, u32[]{:S(2)}, u32[]{:S(2)}) collective-permute-start(bf16[25,2,32,128]{3,2,1,0:T(8,128)(2,1)S(1)} %get-tuple-element.37), channel_id=1, source_target_pairs={{0,64},{256,320},{32,96},{288,352},{1,65},{257,321},{33,97},{289,3... | collective-permute-start | bytes 1228808 | tf_op jit(solution)/shard_map/ppermute | solution.py:378
  51.5 12.4 %collective-permute-start.6 = (bf16[25,2,32,128]{3,2,1,0:T(8,128)(2,1)S(1)}, bf16[25,2,32,128]{3,2,1,0:T(8,128)(2,1)S(1)}, u32[]{:S(2)}, u32[]{:S(2)}) collective-permute-start(bf16[25,2,32,128]{3,2,1,0:T(8,128)(2,1)S(1)} %get-tuple-element.38), channel_id=1, source_target_pairs={{0,192},{256,448},{32,224},{288,480},{1,193},{257,449},{33,225},{2... | collective-permute-start | bytes 1228808 | tf_op jit(solution)/shard_map/ppermute | solution.py:378
  72.4 5.5 %collective-permute-start.11 = (bf16[50,2,32,128]{3,2,1,0:T(8,128)(2,1)S(1)}, bf16[50,2,32,128]{3,2,1,0:T(8,128)(2,1)S(1)}, u32[]{:S(2)}, u32[]{:S(2)}) collective-permute-start(bf16[50,2,32,128]{3,2,1,0:T(8,128)(2,1)S(1)} %get-tuple-element.47.left), channel_id=1, source_target_pairs={{0,32},{32,0},{64,96},{96,64},{128,160},{160,128},{192,224},{224,1... | collective-permute-start | bytes 2457608 | tf_op jit(solution)/shard_map/ppermute | solution.py:400
